TPU v7x, 32 devices: a whole 2x2x4 slice. The times are simulated.
32 devices in a mesh: dp: 8 (over z, y), tensor: 4 (over x, core).
Axes of the slice: x: 2, y: 2, z: 4, core: 2. Of those that a mesh axis runs over, the one named last changes fastest.
Arguments:
- tokens: bfloat16 [12288, 768], P('dp', 'tensor'), may hold values from -6 to 6
- cotangent: bfloat16 [12288, 768], P('dp', 'tensor'), may hold values from -6 to 6
- seq_start: int32 [12288], P('dp'), may hold values from 0 to 384, as said below
- row_place: int32 [8, 1536], P('dp'), may hold values from 0 to 1535, each once within a row
- qkv_weight: bfloat16 [3, 768, 768], P(None, None, 'tensor'), may hold values from -0.21875 to 0.21875
- qv_bias: bfloat16 [2, 768], P(None, 'tensor'), may hold values from -1.5 to 1.5
- out_weight: bfloat16 [768, 768], P('tensor'), may hold values from -0.875 to 0.875
- out_bias: bfloat16 [768], replicated, may hold values from -1.5 to 1.5
- first_gain: bfloat16 [768], replicated, may hold values from 0.5 to 1.5
- first_shift: bfloat16 [768], replicated, may hold values from -1.5 to 1.5
- up_weight: bfloat16 [2, 768, 3072], P(None, None, 'tensor'), may hold values from -0.21875 to 0.21875
- up_bias: bfloat16 [2, 3072], P(None, 'tensor'), may hold values from -1.5 to 1.5
- down_weight: bfloat16 [3072, 768], P('tensor'), may hold values from -0.15625 to 0.15625
- down_bias: bfloat16 [768], replicated, may hold values from -1.5 to 1.5
- second_gain: bfloat16 [768], replicated, may hold values from 0.5 to 1.5
- second_shift: bfloat16 [768], replicated, may hold values from -1.5 to 1.5
Outputs:
- layer_out: bfloat16 [12288, 768], P('dp', 'tensor')
- input_grad: bfloat16 [12288, 768], P('dp', 'tensor')
- qkv_grad: float32 [3, 768, 768], P(None, 'dp', 'tensor')
- qv_bias_grad: float32 [2, 768], P(None, 'tensor')
- out_grad: float32 [768, 768], P('tensor', 'dp')
- out_bias_grad: float32 [768], P('dp')
- first_gain_grad: float32 [768], P('dp')
- first_shift_grad: float32 [768], P('dp')
- up_grad: float32 [2, 768, 3072], P(None, 'dp', 'tensor')
- up_bias_grad: float32 [2, 3072], P(None, 'tensor')
- down_grad: float32 [3072, 768], P('tensor', 'dp')
- down_bias_grad: float32 [768], P('dp')
- second_gain_grad: float32 [768], P('dp')
- second_shift_grad: float32 [768], P('dp')
Inputs may be any that keep to these rules, and one draw needn't show every extreme that they name: seq_start of a token is the offset, within its aligned block of 512 packed rows, of the first token of its sequence; sequences are 128, 256 or 512 tokens long, begin at multiples of 128 and never cross a block. Each row of row_place is a permutation of 0 to 1535.
All inputs are finite; a program needn't handle non-finite values.
Results may differ from a plain program's by a relative error of at most 0.02.
The roundings to bfloat16 on the way count: a program that leaves them out, or rounds other values in their place, can miss the bound.
Values may be sent and summed in bfloat16 or wider, within the bound.
A program may use at most 128 MiB of HBM per device.

v0:
```python
import functools

import jax
import jax.numpy as jnp
from jax import lax
from jax.experimental import pallas as pl
from jax.experimental.pallas import tpu as pltpu
from jax.sharding import PartitionSpec as P

HEADS = 12
HEAD_DIM = 64
BLOCK = 512
BF = jnp.bfloat16
F32 = jnp.float32
MESH = pl.DeviceIdType.MESH
VMEM_LIMIT = 67043328


def dot(a, b, dims):
    return lax.dot_general(a, b, (dims, ((), ())), preferred_element_type=F32)


def place_of():
    me = lax.axis_index("tensor")
    core = me % 2
    side = me // 2
    sibling = side * 2 + (1 - core)
    across = (1 - side) * 2 + core
    diagonal = (1 - side) * 2 + (1 - core)
    return me, sibling, across, diagonal


def enter(devices, groups):
    barrier = pltpu.get_barrier_semaphore()
    count = len(devices)
    for device in devices:
        pl.semaphore_signal(barrier, inc=1, device_id={"tensor": device}, device_id_type=MESH)
    if groups:
        mine = lax.axis_index("dp")

        @pl.loop(1, groups)
        def _(step):
            pl.semaphore_signal(barrier, inc=1, device_id={"dp": (mine + step) % groups}, device_id_type=MESH)

        count += groups - 1
    pl.semaphore_wait(barrier, count)


def send(source, target, send_sem, recv_sem, **where):
    return pltpu.make_async_remote_copy(
        src_ref=source, dst_ref=target, send_sem=send_sem, recv_sem=recv_sem, device_id=where, device_id_type=MESH
    )


def fold_into(buffer, index, values, halves):
    width = values.shape[1]
    if not halves:
        buffer[index] = values
        return
    half = values.shape[0] // 2
    buffer[index + (slice(None), slice(0, width))] = values[:half]
    buffer[index + (slice(None), slice(width, 2 * width))] = values[half:]


def unfold(values, width, halves):
    if not halves:
        return values
    return jnp.concatenate([values[:, :width], values[:, width:]], axis=0)


def call(kernel, number, outs, scratch, args, apart=(), apart_outs=()):
    specs = [pl.BlockSpec(memory_space=pl.ANY if k in apart else pltpu.VMEM) for k in range(len(args))]
    return pl.pallas_call(
        kernel,
        out_shape=outs,
        in_specs=specs,
        out_specs=tuple(
            pl.BlockSpec(memory_space=pl.ANY if k in apart_outs else pltpu.VMEM) for k in range(len(outs))
        ),
        scratch_shapes=scratch,
        compiler_params=pltpu.CompilerParams(
            collective_id=number, has_side_effects=True, vmem_limit_bytes=VMEM_LIMIT
        ),
    )(*args)


def shape(dims, kind):
    return jax.ShapeDtypeStruct(dims, kind)


def to_column(row, column, where):
    for k in range(row.shape[1] // 128):
        piece = jnp.broadcast_to(row[0:1, k * 128 : (k + 1) * 128], (8, 128))
        column[k * 128 : (k + 1) * 128, where : where + 1] = piece.T[:, 0:1]


def slope_of(index):
    value = jnp.float32(2.0 ** (-8.0 / HEADS))
    for head in range(1, HEADS):
        value = jnp.where(index == head, jnp.float32(2.0 ** (-8.0 * (head + 1) / HEADS)), value)
    return value


def key_distance():
    keys = lax.broadcasted_iota(jnp.int32, (BLOCK, BLOCK), 0)
    asks = lax.broadcasted_iota(jnp.int32, (BLOCK, BLOCK), 1)
    return jnp.abs(keys - asks).astype(F32)


def scores_by_key(keys, queries, slope, distance, same):
    raw = dot(keys, queries, ((1,), (1,))) * (HEAD_DIM**-0.5) - slope * distance
    return jnp.where(same, raw, -1e30)


class HeadGather:
    def __init__(self, wide, sems):
        self.wide, self.sems = wide, sems
        self.me, self.sibling, self.across, _ = place_of()

    def copy(self, b, kind, whose, peer):
        return send(self.wide.at[whose, b], self.wide.at[whose, b], self.sems.at[2 * kind, b],
                    self.sems.at[2 * kind + 1, b], tensor=peer)

    def start(self, b, values):
        fold_into(self.wide, (self.me, b), values, True)
        self.copy(b, 0, self.me, self.across).start()
        self.copy(b, 1, self.me, self.sibling).start()

    def relay(self, b):
        self.copy(b, 0, self.me, self.across).wait_recv()
        self.copy(b, 2, self.across, self.sibling).start()

    def land(self, b, out, width):
        self.copy(b, 1, self.me, self.sibling).wait_recv()
        self.copy(b, 2, self.across, self.sibling).wait_recv()
        for s in range(4):
            out[b * BLOCK : (b + 1) * BLOCK, s * width : (s + 1) * width] = unfold(self.wide[s, b], width, True)

    def end(self, b):
        self.copy(b, 0, self.me, self.across).wait_send()
        self.copy(b, 1, self.me, self.sibling).wait_send()
        self.copy(b, 2, self.across, self.sibling).wait_send()


def front_kernel(groups, blocks, tokens, cot, place_row, seq_row, qkv_w, qv_bias, out_w,
                 packed_out, cot_out, full_out, qkv, lse, context, wide_context, taking,
                 tokens_turned, cot_turned, tokens_here, cot_here, weight_here, start_col, chosen, taken, sent, recv, arrived,
                 wide, wide_heads, local_sems, group_sems, gather_sems, head_sems, out_sems):
    me, sibling, across, diagonal = place_of()
    mine = lax.axis_index("dp")
    rows, width = tokens_here.shape
    heads = width // HEAD_DIM
    piece = rows // groups
    halves = (piece // 2) % 8 == 0
    quarter = BLOCK // 4
    loads = [
        pltpu.make_async_copy(source, target, local_sems.at[k])
        for k, (source, target) in enumerate(((tokens, tokens_turned), (cot, cot_turned), (qkv_w, weight_here)))
    ]
    for load in loads:
        load.start()
    enter([sibling, across, diagonal], groups)

    def moved(kind, step):
        peer = (mine + step) % groups
        return send(sent.at[kind, peer], recv.at[kind, mine], group_sems.at[0, kind, step],
                    group_sems.at[1, kind, step], dp=peer)

    def give(kind, source):
        @pl.loop(1, groups)
        def _(step):
            peer = (mine + step) % groups
            values = source[pl.ds(pl.multiple_of(peer * piece, 8), piece), :]
            fold_into(sent, (kind, peer), values, halves)
            moved(kind, step).start()

        values = source[pl.ds(pl.multiple_of(mine * piece, 8), piece), :]
        fold_into(recv, (kind, mine), values, halves)

    loads[0].wait()
    tokens_here[...] = tokens_turned[...].T
    give(0, tokens_here)
    out_far = send(out_w, full_out.at[me], out_sems.at[0], out_sems.at[1], tensor=across)
    out_near = send(out_w, full_out.at[me], out_sems.at[2], out_sems.at[3], tensor=sibling)
    out_pass = send(full_out.at[across], full_out.at[across], out_sems.at[4], out_sems.at[5], tensor=sibling)
    out_far.start()
    out_near.start()
    loads[1].wait()
    cot_here[...] = cot_turned[...].T
    give(1, cot_here)
    full_out[me] = out_w[...]
    to_column(seq_row, start_col, 0)
    for b in range(blocks):
        ids = lax.broadcasted_iota(jnp.int32, (BLOCK, rows), 0) + b * BLOCK
        chosen[b * BLOCK : (b + 1) * BLOCK, :] = jnp.where(ids == place_row[...], 1.0, 0.0).astype(BF)

    to_column(place_row, start_col, 1)
    for b in range(blocks):
        ids = lax.broadcasted_iota(jnp.int32, (BLOCK, rows), 1)
        here = slice(b * BLOCK, (b + 1) * BLOCK)
        taken[here, :] = jnp.where(ids == start_col[here, 1:2], 1.0, 0.0).astype(BF)
    store = pltpu.make_async_copy(taken, taking, local_sems.at[3])
    store.start()

    def placed(b):
        return dot(chosen[b * BLOCK : (b + 1) * BLOCK, :], arrived[...], ((1,), (0,))).astype(BF)

    out_far.wait_recv()
    out_pass.start()

    def land(kind):
        @pl.loop(1, groups)
        def _(step):
            moved(kind, step).wait_recv()

        @pl.loop(0, groups)
        def _(peer):
            arrived[pl.ds(pl.multiple_of(peer * piece, 8), piece), :] = unfold(recv[kind, peer], width, halves)

    token_gather = HeadGather(wide, gather_sems)
    head_gather = HeadGather(wide_heads, head_sems)
    land(0)
    for b in range(blocks):
        token_gather.start(b, placed(b))
        if b >= 1:
            token_gather.relay(b - 1)
    loads[2].wait()

    def attend(b):
        here = slice(b * BLOCK, (b + 1) * BLOCK)
        token_gather.land(b, packed_out, width)
        for k in range(3):
            part = dot(packed_out[here, :], weight_here[k], ((1,), (1,)))
            if k != 1:
                part += qv_bias[k // 2 : k // 2 + 1, :].astype(F32)
            qkv[k, here, :] = part.astype(BF)
        same = start_col[here, 0:1] == seq_row[0:1, here]
        distance = key_distance()
        for h in range(heads):
            lanes = slice(h * HEAD_DIM, (h + 1) * HEAD_DIM)
            scored = scores_by_key(qkv[1, here, lanes], qkv[0, here, lanes], slope_of(me * heads + h), distance, same)
            top = jnp.max(scored, axis=0, keepdims=True)
            raised = jnp.exp(scored - top)
            total = jnp.sum(raised, axis=0, keepdims=True)
            lse[b, h : h + 1, :] = top + jnp.log(total)
            probs = (raised * (1.0 / total)).astype(BF)
            turned = dot(qkv[2, here, lanes].T, probs, ((1,), (0,)))
            context[here, lanes] = turned.T.astype(BF)
        head_gather.start(b, context[here, :])

    for b in range(blocks):
        if b == blocks - 1:
            token_gather.relay(b)
        attend(b)
        if b >= 1:
            head_gather.relay(b - 1)
    for b in range(blocks - 1):
        head_gather.land(b, wide_context, width)
    land(1)
    for b in range(blocks):
        cot_block = placed(b)
        for u in range(4):
            fold_into(cot_out, (u, b), cot_block[u * quarter : (u + 1) * quarter], True)
    head_gather.relay(blocks - 1)
    head_gather.land(blocks - 1, wide_context, width)
    for b in range(blocks):
        token_gather.end(b)
        head_gather.end(b)
    store.wait()
    out_near.wait()
    out_pass.wait()
    out_far.wait_send()
    for kind in range(2):
        @pl.loop(1, groups)
        def _(step):
            moved(kind, step).wait_send()


def front(groups, args, number):
    tokens, qkv_w, out_w = args[0], args[4], args[6]
    width, rows = tokens.shape
    piece = rows // groups
    blocks = rows // BLOCK
    heads = width // HEAD_DIM
    halves = (piece // 2) % 8 == 0
    slab = (2, groups, piece // 2, 2 * width) if halves else (2, groups, piece, width)
    here = pltpu.VMEM((rows, width), BF)
    wide = pltpu.VMEM((4, blocks, BLOCK // 2, 2 * width), BF)
    turned = pltpu.VMEM((width, rows), BF)
    dma = pltpu.SemaphoreType.DMA
    return call(
        functools.partial(front_kernel, groups, blocks),
        number,
        (
            shape((rows, 4 * width), BF),
            shape((4, blocks, BLOCK // 8, 2 * width), BF),
            shape((4,) + out_w.shape, BF),
            shape((3, rows, width), BF),
            shape((blocks, heads, BLOCK), F32),
            shape((rows, width), BF),
            shape((rows, 4 * width), BF),
            shape((rows, rows), BF),
        ),
        [
            turned,
            turned,
            here,
            here,
            pltpu.VMEM(qkv_w.shape, BF),
            pltpu.VMEM((rows, 8), jnp.int32),
            pltpu.VMEM((rows, rows), BF),
            pltpu.VMEM((rows, rows), BF),
            pltpu.VMEM(slab, BF),
            pltpu.VMEM(slab, BF),
            here,
            wide,
            wide,
            dma((4,)),
            dma((2, 2, groups)),
            dma((6, blocks)),
            dma((6, blocks)),
            dma((6,)),
        ],
        args,
        apart=(0, 1, 4),
        apart_outs=(7,),
    )


def norm_unit(values):
    center = values - jnp.mean(values, axis=-1, keepdims=True)
    rs = lax.rsqrt(jnp.mean(center * center, axis=-1, keepdims=True) + 1e-05)
    return center * rs, rs


def norm_back(weighted, unit, rs):
    inner = jnp.mean(weighted * unit, axis=-1, keepdims=True)
    return rs * (weighted - jnp.mean(weighted, axis=-1, keepdims=True) - unit * inner)


class GroupSum:
    def __init__(self, groups, grads, buffers, sems):
        self.acc, self.recv1, self.recv2 = buffers
        self.pair_sems, self.group_sems = sems
        self.grads = grads
        self.pairs = groups // 2
        self.mine = lax.axis_index("dp")
        self.parity = self.mine % 2
        self.pair = self.mine + 1 - 2 * self.parity
        self.slot = self.mine // 2

    def paired(self, kind, step):
        m = (self.slot + step) % self.pairs
        return send(self.grads[kind].at[2 * m + 1 - self.parity], self.recv1.at[kind, m],
                    self.pair_sems.at[0, kind, step], self.pair_sems.at[1, kind, step], dp=self.pair)

    def passed(self, kind, step):
        m = (self.slot + step) % self.pairs
        return send(self.acc.at[kind, m], self.recv2.at[kind, self.slot], self.group_sems.at[0, kind, step],
                    self.group_sems.at[1, kind, step], dp=2 * m + self.parity)

    def start(self, kind):
        @pl.loop(1, self.pairs + 1)
        def _(step):
            self.paired(kind, step).start()

    def forward(self, kinds):
        @pl.loop(1, self.pairs)
        def _(step):
            m = (self.slot + step) % self.pairs
            for kind in kinds:
                self.paired(kind, step).wait_recv()
                own = self.grads[kind][2 * m + self.parity].astype(F32)
                self.acc[kind, m] = (own + self.recv1[kind, m].astype(F32)).astype(BF)
                self.passed(kind, step).start()

    def pair_only(self, kind, shares, own):
        @pl.loop(1, self.pairs)
        def _(step):
            m = (self.slot + step) % self.pairs
            self.paired(kind, step).wait_recv()
            mine = self.grads[kind][2 * m + self.parity].astype(F32)
            shares[m] = (mine + self.recv1[kind, m].astype(F32)).astype(BF)

        self.paired(kind, self.pairs).wait_recv()
        shares[self.slot] = jnp.zeros_like(shares[0])
        own[...] = self.grads[kind][self.mine].astype(F32) + self.recv1[kind, self.slot].astype(F32)

        @pl.loop(1, self.pairs + 1)
        def _(step):
            self.paired(kind, step).wait_send()

    def collect(self, kind):
        self.paired(kind, self.pairs).wait_recv()
        total = self.grads[kind][self.mine].astype(F32) + self.recv1[kind, self.slot].astype(F32)
        for step in range(1, self.pairs):
            self.passed(kind, step).wait_recv()
            total += self.recv2[kind, (self.slot + self.pairs - step) % self.pairs].astype(F32)
        return total

    def end(self, kinds):
        for kind in kinds:
            @pl.loop(1, self.pairs + 1)
            def _(step):
                self.paired(kind, step).wait_send()

            @pl.loop(1, self.pairs)
            def _(step):
                self.passed(kind, step).wait_send()

    @staticmethod
    def scratch(kinds, groups, held, span):
        exchange = pltpu.VMEM((kinds, groups // 2, held, span), BF)
        sems = pltpu.SemaphoreType.DMA((2, kinds, groups // 2 + 1))
        return [exchange] * 3 + [sems] * 2


class ShareSum:
    def __init__(self, groups, shares, recv, sems):
        self.shares, self.recv, self.sems = shares, recv, sems
        self.pairs = groups // 2
        mine = lax.axis_index("dp")
        self.parity, self.slot = mine % 2, mine // 2

    def passed(self, step):
        m = (self.slot + step) % self.pairs
        return send(self.shares.at[m], self.recv.at[self.slot], self.sems.at[0, step], self.sems.at[1, step],
                    dp=2 * m + self.parity)

    def start(self):
        @pl.loop(1, self.pairs)
        def _(step):
            self.passed(step).start()

    def collect(self, own):
        total = own[...]
        for step in range(1, self.pairs):
            self.passed(step).wait()
            total += self.recv[(self.slot + self.pairs - step) % self.pairs].astype(F32)
        return total


class GiveBack:
    def __init__(self, groups, rows, width, chosen, sent, recv, sems):
        self.groups, self.piece, self.width = groups, rows // groups, width
        self.halves = (self.piece // 2) % 8 == 0
        self.chosen, self.sent, self.recv, self.sems = chosen, sent, recv, sems
        self.mine = lax.axis_index("dp")

    def moved(self, step):
        peer = (self.mine + step) % self.groups
        return send(self.sent.at[peer], self.recv.at[self.mine], self.sems.at[0, step], self.sems.at[1, step], dp=peer)

    def start(self, packed):
        @pl.loop(0, self.groups)
        def _(step):
            peer = (self.mine + step) % self.groups
            rows = self.chosen[pl.ds(pl.multiple_of(peer * self.piece, 8), self.piece), :]
            values = dot(rows, packed[...], ((1,), (0,))).astype(BF)

            @pl.when(step > 0)
            def _():
                fold_into(self.sent, (peer,), values, self.halves)
                self.moved(step).start()

            @pl.when(step == 0)
            def _():
                fold_into(self.recv, (self.mine,), values, self.halves)

    def land(self, target):
        @pl.loop(1, self.groups)
        def _(step):
            self.moved(step).wait_recv()

        @pl.loop(0, self.groups)
        def _(peer):
            here = pl.ds(pl.multiple_of(peer * self.piece, 8), self.piece)
            target[here, :] = unfold(self.recv[peer], self.width, self.halves)

        @pl.loop(1, self.groups)
        def _(step):
            self.moved(step).wait_send()

    @staticmethod
    def scratch(groups, rows, width):
        piece = rows // groups
        halves = (piece // 2) % 8 == 0
        slab = (groups, piece // 2, 2 * width) if halves else (groups, piece, width)
        return [pltpu.VMEM(slab, BF)] * 2 + [pltpu.SemaphoreType.DMA((2, groups))]


class RowSum:
    def __init__(self, part, first, second, third, sems):
        self.part, self.first, self.second, self.third, self.sems = part, first, second, third, sems
        self.me, self.sibling, self.across, self.diagonal = place_of()

    def cross(self, b):
        return send(self.part.at[b, self.diagonal], self.first.at[b], self.sems.at[0, b], self.sems.at[1, b],
                    tensor=self.sibling)

    def near(self, b):
        return send(self.part.at[b, self.sibling], self.second.at[b], self.sems.at[2, b], self.sems.at[3, b],
                    tensor=self.sibling)

    def far(self, b):
        return send(self.first.at[b], self.third.at[b], self.sems.at[4, b], self.sems.at[5, b], tensor=self.across)

    def start(self, b):
        self.cross(b).start()
        self.near(b).start()

    def relay(self, b):
        self.cross(b).wait()
        self.first[b] = (self.part[b, self.across].astype(F32) + self.first[b].astype(F32)).astype(BF)
        self.far(b).start()

    def total(self, b):
        self.near(b).wait()
        self.far(b).wait()
        return self.part[b, self.me].astype(F32) + self.second[b].astype(F32) + self.third[b].astype(F32)

    @staticmethod
    def scratch(blocks, rows, columns):
        buffer = pltpu.VMEM((blocks, rows, columns), BF)
        return [pltpu.VMEM((blocks, 4, rows, columns), BF)] + [buffer] * 3 + [pltpu.SemaphoreType.DMA((6, blocks))]


class RowGather:
    def __init__(self, out, sems):
        self.out, self.sems = out, sems
        self.me, self.sibling, self.across, _ = place_of()

    def copy(self, b, kind, whose, peer):
        return send(self.out.at[b, whose], self.out.at[b, whose], self.sems.at[2 * kind, b],
                    self.sems.at[2 * kind + 1, b], tensor=peer)

    def start(self, b):
        self.copy(b, 0, self.me, self.across).start()
        self.copy(b, 1, self.me, self.sibling).start()

    def relay(self, b):
        self.copy(b, 0, self.me, self.across).wait_recv()
        self.copy(b, 2, self.across, self.sibling).start()

    def land(self, b):
        self.copy(b, 1, self.me, self.sibling).wait_recv()
        self.copy(b, 2, self.across, self.sibling).wait_recv()

    def end(self, b):
        self.copy(b, 0, self.me, self.across).wait_send()
        self.copy(b, 1, self.me, self.sibling).wait_send()
        self.copy(b, 2, self.across, self.sibling).wait_send()


CHUNK = 256


def mid_kernel(groups, blocks, grad_scale, context, packed, full_out, up_w, up_bias, down_w, cot_folded, v0, v1, v2, v3, v4, v5,
               d_low, d_own, small, value_grad, down_grad, gate_shares, gate_sum, folded,
               normed_low, slope_term, gelu_term, gated, d_gate, d_value, unit_full, rs_full, unit_own, rs_own, d_mixed,
               mixed, whole_grad, down_pieces, gate_pieces, cot_recv,
               part1, first1, second1, third1, sems1, part2, first2, second2, third2, sems2, sems3, sems4, c_sems,
               vector_rows, acc, recv1, recv2, pair_sems, group_sems):
    me, sibling, across, diagonal = place_of()
    columns = packed.shape[1]
    width = columns // 4
    quarter = BLOCK // 4
    held = down_pieces.shape[1]
    enter([sibling, across, diagonal], groups)
    swaps = [
        send(cot_folded.at[peer], cot_recv.at[me], c_sems.at[0, k], c_sems.at[1, k], tensor=peer)
        for k, peer in enumerate((across, diagonal, sibling))
    ]
    for swap in swaps:
        swap.start()
    cot_recv[me] = cot_folded[me]
    ffn = RowSum(part1, first1, second1, third1, sems1)
    back_sum = RowSum(part2, first2, second2, third2, sems2)
    mixed_gather = RowGather(mixed, sems3)
    hidden_gather = RowGather(d_low, sems4)
    sums = GroupSum(groups, (down_pieces, gate_pieces), (acc, recv1, recv2), (pair_sems, group_sems))
    small[...] = jnp.zeros_like(small)
    for k, vector in enumerate((v0, v1, v2, v3, v4, v5)):
        vector_rows[k : k + 1, :] = vector[...].astype(F32).reshape(1, columns)
    out_bias, first_gain, first_shift, down_bias, second_gain, second_shift = (
        vector_rows.at[k : k + 1] for k in range(6)
    )

    def add_small(row, values):
        small[row : row + 1, :] += jnp.sum(values, axis=0, keepdims=True) * grad_scale

    def ahead(b, c):
        here = slice(b * BLOCK + c * CHUNK, b * BLOCK + (c + 1) * CHUNK)
        inner = slice(c * CHUNK, (c + 1) * CHUNK)
        hidden = packed[here, :].astype(F32) + (dot(context[here, :], full_out[...], ((1,), (0,))) + out_bias[...])
        unit, rs = norm_unit(hidden)
        unit_full[inner, :] = unit
        rs_full[inner, :] = rs
        low = (unit * first_gain[...] + first_shift[...]).astype(BF)
        normed_low[here, :] = low
        gate = dot(low, up_w[0], ((1,), (0,))) + up_bias[0:1, :].astype(F32)
        value = dot(low, up_w[1], ((1,), (0,))) + up_bias[1:2, :].astype(F32)
        half_erf = 0.5 * (1.0 + lax.erf(gate * (0.5**0.5)))
        gelu = gate * half_erf
        slope = half_erf + gate * jnp.exp(-0.5 * gate * gate) * ((2.0 * jnp.pi) ** (-0.5))
        slope_term[here, :] = value * slope
        gelu_term[here, :] = gelu
        low_gated = (gelu * value).astype(BF)
        gated[here, :] = low_gated
        out = dot(low_gated, down_w[...], ((1,), (0,))).astype(BF)
        for k in range(CHUNK // quarter):
            part1[b, c * (CHUNK // quarter) + k] = out[k * quarter : (k + 1) * quarter]

    def keep_own(b):
        mine = pl.ds(pl.multiple_of(me * quarter, quarter), quarter)
        unit_own[b] = unit_full[mine, :]
        rs_own[b] = rs_full[mine, :]
        ffn.start(b)

    def turn(b):
        if b == 0:
            for swap in swaps:
                swap.wait_recv()
        values = unit_own[b] * first_gain[...] + first_shift[...] + (ffn.total(b) + down_bias[...])
        unit, rs = norm_unit(values)
        out = (unit * second_gain[...] + second_shift[...]).astype(BF)
        for u in range(4):
            fold_into(folded, (u, b), out[:, u * width : (u + 1) * width], True)
        cot_rows = jnp.concatenate([unfold(cot_recv[s, b], width, True) for s in range(4)], axis=1).astype(F32)
        d_rows = norm_back(cot_rows * second_gain[...], unit, rs)
        d_mixed[b] = d_rows
        mixed[b, me] = d_rows.astype(BF)
        mixed_gather.start(b)
        add_small(3, d_rows)
        add_small(4, cot_rows * unit)
        add_small(5, cot_rows)

    def astern(b):
        mixed_gather.land(b)
        for c in range(BLOCK // CHUNK):
            here = slice(b * BLOCK + c * CHUNK, b * BLOCK + (c + 1) * CHUNK)
            count = CHUNK // quarter
            d_rows = jnp.concatenate([mixed[b, c * count + k] for k in range(count)], axis=0)
            d_gated = dot(d_rows, down_w[...], ((1,), (1,)))
            gate_rows = (d_gated * slope_term[here, :]).astype(BF)
            value_rows = (d_gated * gelu_term[here, :]).astype(BF)
            d_gate[here, :] = gate_rows
            d_value[here, :] = value_rows
            add_small(8, gate_rows.astype(F32))
            add_small(9, value_rows.astype(F32))
            out = dot(gate_rows, up_w[0], ((1,), (1,))) + dot(value_rows, up_w[1], ((1,), (1,)))
            out = out.astype(BF)
            for k in range(count):
                part2[b, c * count + k] = out[k * quarter : (k + 1) * quarter]
        back_sum.start(b)

    def finish(b):
        d_normed = d_mixed[b] + back_sum.total(b)
        d_hidden = norm_back(d_normed * first_gain[...], unit_own[b], rs_own[b])
        d_own[b] = d_hidden
        d_low[b, me] = d_hidden.astype(BF)
        hidden_gather.start(b)
        add_small(0, d_hidden)
        add_small(1, d_normed * unit_own[b])
        add_small(2, d_normed)

    def weight_grad(left, right, pieces):
        span = right.shape[1]
        for c in range(span // CHUNK):
            lanes = slice(c * CHUNK, (c + 1) * CHUNK)
            whole_grad[:, lanes] = dot(left, right[:, lanes], ((0,), (0,)))
        for g in range(groups):
            pieces[g] = (whole_grad[g * held : (g + 1) * held, :] * grad_scale).astype(BF)

    last = blocks - 1
    for b in range(blocks):
        ahead(b, 0)
        if b >= 1:
            ffn.relay(b - 1)
        if b >= 2:
            turn(b - 2)
        ahead(b, 1)
        keep_own(b)
        if b >= 2:
            mixed_gather.relay(b - 2)
    ffn.relay(last)
    if blocks > 1:
        turn(last - 1)
    turn(last)
    if blocks > 1:
        mixed_gather.relay(last - 1)
    for b in range(blocks):
        if b == last:
            mixed_gather.relay(last)
        astern(b)
        if b >= 1:
            back_sum.relay(b - 1)
    back_sum.relay(last)
    d_mixed_rows = jnp.concatenate([mixed[b, k] for b in range(blocks) for k in range(4)], axis=0)
    weight_grad(d_mixed_rows, gated, down_pieces)
    sums.start(0)
    finish(0)
    weight_grad(normed_low[...], d_gate, gate_pieces)
    sums.start(1)
    if blocks > 1:
        finish(1)
    weight_grad(normed_low[...], d_value, value_grad)
    for b in range(2, blocks):
        finish(b)
    for b in range(blocks):
        hidden_gather.relay(b)
    sums.forward((0,))
    for b in range(blocks):
        hidden_gather.land(b)
    sums.pair_only(1, gate_shares, gate_sum)
    down_grad[...] = sums.collect(0)
    for b in range(blocks):
        mixed_gather.end(b)
        hidden_gather.end(b)
    for swap in swaps:
        swap.wait_send()
    sums.end((0,))


def mid(groups, grad_scale, args, number):
    context, up_w, cot_folded = args[0], args[3], args[6]
    rows, columns = context.shape
    units = up_w.shape[2]
    held = columns // groups
    blocks = rows // BLOCK
    quarter = BLOCK // 4
    own = (blocks, quarter, columns)
    dma = pltpu.SemaphoreType.DMA
    outs = (
        shape((blocks, 4, quarter, columns), BF),
        shape(own, F32),
        shape((16, columns), F32),
        shape((groups, held, units), BF),
        shape((held, units), F32),
        shape((groups // 2, held, units), BF),
        shape((held, units), F32),
        shape(cot_folded.shape, BF),
    )
    return call(
        functools.partial(mid_kernel, groups, blocks, grad_scale),
        number,
        outs,
        [
            pltpu.VMEM((rows, columns), BF),
            pltpu.VMEM((rows, units), F32),
            pltpu.VMEM((rows, units), F32),
            pltpu.VMEM((rows, units), BF),
            pltpu.VMEM((rows, units), BF),
            pltpu.VMEM((rows, units), BF),
            pltpu.VMEM((BLOCK, columns), F32),
            pltpu.VMEM((BLOCK, 1), F32),
            pltpu.VMEM(own, F32),
            pltpu.VMEM((blocks, quarter, 1), F32),
            pltpu.VMEM(own, F32),
            pltpu.VMEM((blocks, 4, quarter, columns), BF),
            pltpu.VMEM((columns, units), F32),
            pltpu.VMEM((groups, held, units), BF),
            pltpu.VMEM((groups, held, units), BF),
            pltpu.VMEM(cot_folded.shape, BF),
        ]
        + RowSum.scratch(blocks, quarter, columns)
        + RowSum.scratch(blocks, quarter, columns)
        + [dma((6, blocks)), dma((6, blocks)), dma((2, 3)), pltpu.VMEM((6, columns), F32)]
        + GroupSum.scratch(2, groups, held, units),
        args,
    )


def back_kernel(groups, blocks, grad_scale, dh_low, dh_own, qkv, lse, seq_row, context, packed_in, qkv_w,
                out_w, value_grad, gate_shares, gate_sum, folded, small, taking,
                layer_out, input_grad, up_grad, qkv_grad, out_grad, small_out,
                d_rows, d_part, late_sum, late, cols, one, two, three, packed, ssent, srecv, swide, x_sems, s_sems, w_sems,
                start_col, chosen, weight_here, returned, landed, load_sem, r_sems,
                acc, recv1, recv2, pair_sems, group_sems, acc2, recv3, recv4, pair_sems2, group_sems2, share_recv, share_sems,
                sent, recv, a_sems, sent2, recv5, a_sems2):
    me, sibling, across, diagonal = place_of()
    mine = lax.axis_index("dp")
    width, rows = input_grad.shape
    heads = width // HEAD_DIM
    held = late.shape[1]
    quarter = BLOCK // 4
    load = pltpu.make_async_copy(qkv_w, weight_here, load_sem.at[0])
    load.start()
    load_rows = pltpu.make_async_copy(taking, chosen, load_sem.at[1])
    load_rows.start()
    enter([sibling, across, diagonal], groups)
    sums = GroupSum(groups, (value_grad,), (acc, recv1, recv2), (pair_sems, group_sems))
    late_sums = GroupSum(groups, (late,), (acc2, recv3, recv4), (pair_sems2, group_sems2))
    giving = GiveBack(groups, rows, width, chosen, sent, recv, a_sems)
    giving_result = GiveBack(groups, rows, width, chosen, sent2, recv5, a_sems2)
    gate = ShareSum(groups, gate_shares, share_recv, share_sems)
    gate.start()
    sums.start(0)
    returns = [
        send(folded.at[peer], returned.at[me], r_sems.at[0, k], r_sems.at[1, k], tensor=peer)
        for k, peer in enumerate((across, diagonal, sibling))
    ]
    for swap in returns:
        swap.start()
    returned[me] = folded[me]
    def cross(b):
        return send(cols.at[diagonal, b], one.at[b], x_sems.at[0, b], x_sems.at[1, b], tensor=sibling)

    def near(b):
        return send(cols.at[sibling, b], two.at[b], x_sems.at[2, b], x_sems.at[3, b], tensor=sibling)

    def far(b):
        return send(one.at[b], three.at[b], x_sems.at[4, b], x_sems.at[5, b], tensor=across)

    def relay(b):
        cross(b).wait()
        one[b] = (cols[across, b].astype(F32) + one[b].astype(F32)).astype(BF)
        far(b).start()

    to_column(seq_row, start_col, 0)
    late_sum[:, 3 * width :] = dot(dh_low[...], context[...], ((0,), (0,)))
    load.wait()
    ssent[...] = small[...]

    @pl.loop(0, blocks)
    def _(b):
        here = pl.ds(pl.multiple_of(b * BLOCK, BLOCK), BLOCK)
        dh = dh_low[here, :]
        d_context = dot(dh, out_w[...], ((1,), (1,))).astype(BF)
        same = start_col[here, 0:1] == seq_row[0:1, here]
        distance = key_distance()
        for h in range(heads):
            lanes = slice(h * HEAD_DIM, (h + 1) * HEAD_DIM)
            queries = qkv[0, here, lanes]
            keys = qkv[1, here, lanes]
            values = qkv[2, here, lanes]
            d_rows_out = d_context[:, lanes]
            scored = scores_by_key(keys, queries, slope_of(me * heads + h), distance, same)
            probs = jnp.exp(scored - lse[b, h : h + 1, :])
            d_probs = dot(values, d_rows_out, ((1,), (1,)))
            d_rows[2, here, lanes] = dot(probs.astype(BF), d_rows_out, ((1,), (0,))).astype(BF)
            center = jnp.sum(probs * d_probs, axis=0, keepdims=True)
            d_scores = (probs * (d_probs - center)).astype(BF)
            d_rows[1, here, lanes] = (dot(d_scores, queries, ((1,), (0,))) * (HEAD_DIM**-0.5)).astype(BF)
            turned = dot(keys.T, d_scores, ((1,), (0,))) * (HEAD_DIM**-0.5)
            d_rows[0, here, lanes] = turned.T.astype(BF)
        part = dot(d_rows[0, here, :], weight_here[0], ((1,), (0,)))
        part += dot(d_rows[1, here, :], weight_here[1], ((1,), (0,)))
        part += dot(d_rows[2, here, :], weight_here[2], ((1,), (0,)))
        d_part[...] = part
        d_part[pl.ds(pl.multiple_of(me * quarter, quarter), quarter), :] += dh_own[b]
        for u in range(4):
            fold_into(cols, (u, b), d_part[:, u * width : (u + 1) * width].astype(BF), True)
        cross(b).start()
        near(b).start()
        last = small.shape[0] - 6
        for k, c in enumerate((0, 2)):
            bias = jnp.sum(d_rows[c, here, :].astype(F32), axis=0, keepdims=True) * grad_scale
            ssent[last : last + 1, k * 2 * 128 : k * 2 * 128 + width] += bias
        relay(b)

        @pl.when(b == 0)
        def _():
            sums.forward((0,))

        @pl.when(b == 1)
        def _():
            load_rows.wait()
            for swap in returns:
                swap.wait_recv()
            for q in range(blocks):
                for s in range(4):
                    start = q * BLOCK + s * quarter
                    packed[start : start + quarter, :] = unfold(returned[s, q], width, True)
            giving_result.start(packed)

    for c in range(3):
        late_sum[:, c * width : (c + 1) * width] = dot(packed_in[...], d_rows[c], ((0,), (0,)))
    for g in range(groups):
        late[g] = (late_sum[g * held : (g + 1) * held, :] * grad_scale).astype(BF)

    late_sums.start(0)
    swaps = [
        send(ssent, srecv.at[me], s_sems.at[0, k], s_sems.at[1, k], tensor=peer)
        for k, peer in enumerate((sibling, across, diagonal))
    ]
    for swap in swaps:
        swap.start()
    srecv[me] = ssent[...]

    for b in range(blocks):
        near(b).wait()
        far(b).wait_recv()
        total = cols[me, b].astype(F32) + two[b].astype(F32) + three[b].astype(F32)
        packed[b * BLOCK : (b + 1) * BLOCK, :] = unfold(total.astype(BF), width, True)
    giving.start(packed)

    for swap in swaps:
        swap.wait_recv()
    shared = small.shape[0] // 2
    swide[mine, 0:shared] = srecv[0, 0:shared] + srecv[1, 0:shared] + srecv[2, 0:shared] + srecv[3, 0:shared]
    swide[mine, shared:] = ssent[shared:, :]

    def spread(step):
        peer = (mine + step) % groups
        return send(swide.at[mine], swide.at[mine], w_sems.at[0, step], w_sems.at[1, step], dp=peer)

    @pl.loop(1, groups)
    def _(step):
        spread(step).start()

    late_sums.forward((0,))
    up_grad[0] = gate.collect(gate_sum)
    up_grad[1] = sums.collect(0)
    giving_result.land(landed)
    layer_out[...] = landed[...].T

    @pl.loop(1, groups)
    def _(step):
        spread(step).wait_recv()

    small_out[...] = swide[0]

    @pl.loop(1, groups)
    def _(peer):
        small_out[...] += swide[peer]

    total = late_sums.collect(0)
    for c in range(3):
        qkv_grad[c] = total[:, c * width : (c + 1) * width]
    out_grad[...] = total[:, 3 * width :].T
    giving.land(landed)
    input_grad[...] = landed[...].T
    for b in range(blocks):
        far(b).wait_send()
    for copy in swaps + returns:
        copy.wait_send()
    sums.end((0,))
    late_sums.end((0,))

    @pl.loop(1, groups)
    def _(step):
        spread(step).wait_send()


def back(groups, grad_scale, args, small, number):
    dh_low, qkv, qkv_w, grad, folded = args[0], args[2], args[7], args[9], args[12]
    rows, columns = dh_low.shape
    width = qkv.shape[2]
    held, units = grad.shape[1:]
    blocks = rows // BLOCK
    half = (blocks, BLOCK // 2, 2 * width)
    dma = pltpu.SemaphoreType.DMA
    outs = (
        shape((width, rows), BF),
        shape((width, rows), BF),
        shape((2, held, units), F32),
        shape((3, held, width), F32),
        shape((width, held), F32),
        shape(small.shape, F32),
    )
    return call(
        functools.partial(back_kernel, groups, blocks, grad_scale),
        number,
        outs,
        [
            pltpu.VMEM((3, rows, width), BF),
            pltpu.VMEM((BLOCK, columns), F32),
            pltpu.VMEM((columns, 4 * width), F32),
            pltpu.VMEM((groups, held, 4 * width), BF),
            pltpu.VMEM((4,) + half, BF),
            pltpu.VMEM(half, BF),
            pltpu.VMEM(half, BF),
            pltpu.VMEM(half, BF),
            pltpu.VMEM((rows, width), BF),
            pltpu.VMEM(small.shape, F32),
            pltpu.VMEM((4,) + small.shape, F32),
            pltpu.VMEM((groups,) + small.shape, F32),
            dma((6, blocks)),
            dma((2, 3)),
            dma((2, groups)),
            pltpu.VMEM((rows, 8), jnp.int32),
            pltpu.VMEM((rows, rows), BF),
            pltpu.VMEM(qkv_w.shape, BF),
            pltpu.VMEM(folded.shape, BF),
            pltpu.VMEM((rows, width), BF),
            dma((2,)),
            dma((2, 3)),
        ]
        + GroupSum.scratch(1, groups, held, units)
        + GroupSum.scratch(1, groups, held, 4 * width)
        + [pltpu.VMEM((groups // 2, held, units), BF), dma((2, groups // 2))]
        + GiveBack.scratch(groups, rows, width)
        + GiveBack.scratch(groups, rows, width),
        args,
        apart=(7, 14),
    )


def on_device(
    tokens,
    cotangent,
    seq_start,
    row_place,
    qkv_weight,
    qv_bias,
    out_weight,
    out_bias,
    first_gain,
    first_shift,
    up_weight,
    up_bias,
    down_weight,
    down_bias,
    second_gain,
    second_shift,
):
    row_count, width = tokens.shape
    columns = qkv_weight.shape[1]
    groups = lax.axis_size("dp")
    grad_scale = (row_count * groups) ** (-0.5)
    seq_row = seq_start.reshape(1, row_count)
    weight_turned = qkv_weight.transpose(0, 2, 1)
    packed_in, cot_folded, full_out, qkv_rows, log_total, context, wide_context, taking = front(
        groups, (tokens.T, cotangent.T, row_place, seq_row, weight_turned, qv_bias, out_weight), 0
    )
    d_low, d_own, small, value_grad, down_grad, gate_shares, gate_sum, folded = mid(
        groups,
        grad_scale,
        (
            wide_context,
            packed_in,
            full_out.reshape(columns, columns),
            up_weight,
            up_bias,
            down_weight,
            cot_folded,
            out_bias,
            first_gain,
            first_shift,
            down_bias,
            second_gain,
            second_shift,
        ),
        1,
    )
    layer_out, input_grad, up_grad, qkv_grad, out_grad, sums = back(
        groups,
        grad_scale,
        (
            d_low.reshape(row_count, columns),
            d_own,
            qkv_rows,
            log_total,
            seq_row,
            context,
            packed_in,
            weight_turned,
            out_weight,
            value_grad,
            gate_shares,
            gate_sum,
            folded,
            small,
            taking,
        ),
        small,
        2,
    )
    rows_here = columns // groups
    sums_here = lax.dynamic_slice_in_dim(sums[:6], lax.axis_index("dp") * rows_here, rows_here, 1)
    return (
        layer_out.T,
        input_grad.T,
        qkv_grad,
        jnp.stack([sums[10, :width], sums[10, 256 : 256 + width]]),
        out_grad,
        sums_here[0],
        sums_here[1],
        sums_here[2],
        up_grad,
        sums[8:10],
        down_grad.T,
        sums_here[3],
        sums_here[4],
        sums_here[5],
    )


def solution(mesh):
    return jax.shard_map(
        on_device,
        mesh=mesh,
        in_specs=(
            P("dp", "tensor"),
            P("dp", "tensor"),
            P("dp"),
            P("dp", None),
            P(None, None, "tensor"),
            P(None, "tensor"),
            P("tensor", None),
            P(),
            P(),
            P(),
            P(None, None, "tensor"),
            P(None, "tensor"),
            P("tensor", None),
            P(),
            P(),
            P(),
        ),
        out_specs=(
            P("dp", "tensor"),
            P("dp", "tensor"),
            P(None, "dp", "tensor"),
            P(None, "tensor"),
            P("tensor", "dp"),
            P("dp"),
            P("dp"),
            P("dp"),
            P(None, "dp", "tensor"),
            P(None, "tensor"),
            P("tensor", "dp"),
            P("dp"),
            P("dp"),
            P("dp"),
        ),
        check_vma=False,
    )
```

profile of v0, /device:TPU:0, one launch (start us, length us, event | category | flops | bytes accessed | tf_op | source)
XLA Modules:
  0.0 246.0 jit_solution(8942334488068702944)
XLA Ops:
  0.6 1.3 reshape.37.seq_row
  1.9 55.9 %shard_map.263 = (bf16[1536,768]{1,0:T(8,128)(2,1)}, bf16[4,3,64,384]{3,2,1,0:T(8,128)(2,1)}, bf16[4,192,768]{2,1,0:T(8,128)(2,1)}, bf16[3,1536,192]{2,1,0:T(8,1...) custom-call(bf16[192,1536]{1,0:T(8,128)(2,1)} %bitcast.26, ...), custom_call_target="tpu_custom_call" | custom-call | tf_op jit(solution)/shard_map/pallas_call | solution.py:73
  57.8 93.5 %shard_map.264 = (bf16[3,4,128,768]{3,2,1,0:T(8,128)(2,1)}, f32[3,128,768]{2,1,0:T(8,128)}, f32[16,768]{1,0:T(8,128)}, bf16[8,96,768]{2,1,0:T(8,128)(2,1)}, f32[...) custom-call(bf16[1536,768]{1,0:T(8,128)(2,1)} %get-tuple-element.36.context, ...), custom_call_target="tpu_custom_call" | custom-call | tf_op jit(solution)/shard_map/pallas_call | solution.py:73
  151.3 83.6 %shard_map.265 = (bf16[192,1536]{1,0:T(8,128)(2,1)}, bf16[192,1536]{1,0:T(8,128)(2,1)}, f32[2,96,768]{2,1,0:T(8,128)}, f32[3,96,192]{2,1,0:T(8,128)}, f32[192,96]{1,0:T(8,128)}, /*index=5*/f32[16,768]{1,0:T(8,128)}) custom-call(bf16[1536,768]{1,0:T(8,128)(2,1)} %bitcast.22, f32[3,128,768]{2,1,0:T(8,128)} %get-tuple-element.41.dh_own, ...), custom_call_target="tpu_custom_call" | custom-call | tf_op jit(solution)/shard_map/pallas_call | solution.py:73
  234.9 0.0 copy-start.2
  234.9 0.0 copy-start.3
  235.0 0.0 copy-start
  235.0 0.0 copy-start.1
  235.0 0.8 fusion
  235.8 0.6 pad_maximum_fusion
  236.4 0.7 slice.32
  237.1 0.1 constant_dynamic-slice_fusion
  237.2 0.5 slice_bitcast_fusion
  237.7 1.3 slice.36
  239.1 1.9 copy.36
  241.0 1.9 copy.37
  242.9 0.0 copy-done.2
  242.9 0.7 copy.38
  243.6 0.0 copy-done.3
  243.6 0.6 copy.39
  244.3 0.0 copy-done
  244.3 0.8 copy.40
  245.1 0.0 copy-done.1
  245.1 0.7 copy.41
Async XLA Ops:
  234.9 8.0 %copy-start.2 = (f32[3,96,192]{2,1,0:T(8,128)S(1)}, f32[3,96,192]{2,1,0:T(8,128)}, u32[]{:S(2)}) copy-start(f32[3,96,192]{2,1,0:T(8,128)} %get-tuple-element.82) | copy-start | bytes 663556
  234.9 8.7 %copy-start.3 = (f32[192,96]{1,0:T(8,128)S(1)}, f32[192,96]{1,0:T(8,128)}, u32[]{:S(2)}) copy-start(f32[192,96]{1,0:T(8,128)} %get-tuple-element.84) | copy-start | bytes 221188
  235.0 9.3 %copy-start = (f32[2,96,768]{2,1,0:T(8,128)S(1)}, f32[2,96,768]{2,1,0:T(8,128)}, u32[]{:S(2)}) copy-start(f32[2,96,768]{2,1,0:T(8,128)} %get-tuple-element.88) | copy-start | bytes 1769476
  235.0 10.1 %copy-start.1 = (f32[96,768]{1,0:T(8,128)S(1)}, f32[96,768]{1,0:T(8,128)}, u32[]{:S(2)}) copy-start(f32[96,768]{1,0:T(8,128)} %get-tuple-element.57) | copy-start | bytes 884740
where the time goes:
time: 250 us; the launch traced here: 246 us
  Pallas kernels  233 us (93%)
  local copies, waits for them, and re-layouts  11.5 us (5%)
    pallas_call x3, Pallas kernels, call(): pl.pallas_call(kernel, out_shape=outs, in_specs=specs, out_specs=tuple((p...  233 us
    unnamed x14, local copies, waits for them, and re-layouts  6.73 us

commit v1 on v0

--- a/solution.py
+++ b/solution.py
@@ -339,105 +339,74 @@
 
 
 class GroupSum:
-    def __init__(self, groups, grads, buffers, sems):
-        self.acc, self.recv1, self.recv2 = buffers
-        self.pair_sems, self.group_sems = sems
-        self.grads = grads
-        self.pairs = groups // 2
+    def __init__(self, groups, grads, scratch):
+        self.groups, self.grads = groups, grads
+        self.stages = groups.bit_length() - 1
+        self.recv = scratch[: self.stages]
+        self.held = (None,) + tuple(scratch[self.stages : 2 * self.stages - 1])
+        self.sems = scratch[-1]
         self.mine = lax.axis_index("dp")
-        self.parity = self.mine % 2
-        self.pair = self.mine + 1 - 2 * self.parity
-        self.slot = self.mine // 2
-
-    def paired(self, kind, step):
-        m = (self.slot + step) % self.pairs
-        return send(self.grads[kind].at[2 * m + 1 - self.parity], self.recv1.at[kind, m],
-                    self.pair_sems.at[0, kind, step], self.pair_sems.at[1, kind, step], dp=self.pair)
-
-    def passed(self, kind, step):
-        m = (self.slot + step) % self.pairs
-        return send(self.acc.at[kind, m], self.recv2.at[kind, self.slot], self.group_sems.at[0, kind, step],
-                    self.group_sems.at[1, kind, step], dp=2 * m + self.parity)
+
+    def count(self, stage):
+        return self.groups >> (stage + 1)
+
+    def index(self, stage, step):
+        return (self.mine // (2 << stage) + step) % self.count(stage)
+
+    def given(self, stage, step):
+        bit = (self.mine // (1 << stage)) % 2
+        low = self.mine % (1 << stage)
+        return self.index(stage, step) * (2 << stage) + (1 - bit) * (1 << stage) + low
+
+    def copy(self, kind, stage, step):
+        bit = (self.mine // (1 << stage)) % 2
+        partner = self.mine + (1 - 2 * bit) * (1 << stage)
+        at = self.index(stage, step)
+        source = self.held[stage].at[kind, at] if stage else self.grads[kind].at[self.given(0, step)]
+        return send(source, self.recv[stage].at[kind, at], self.sems.at[0, kind, stage, step],
+                    self.sems.at[1, kind, stage, step], dp=partner)
 
     def start(self, kind):
-        @pl.loop(1, self.pairs + 1)
+        @pl.loop(1, self.count(0) + 1)
         def _(step):
-            self.paired(kind, step).start()
-
-    def forward(self, kinds):
-        @pl.loop(1, self.pairs)
+            self.copy(kind, 0, step).start()
+
+    def total(self, kind, stages, piece):
+        total = self.grads[kind][piece].astype(F32)
+        for stage in range(stages):
+            count = self.count(stage)
+            at = piece // (2 << stage)
+            step = (at + 2 * count - 1 - self.mine // (2 << stage)) % count + 1
+            self.copy(kind, stage, step).wait_recv()
+            total += self.recv[stage][kind, at].astype(F32)
+        return total
+
+    def stage(self, kind, stage):
+        @pl.loop(1, self.count(stage) + 1)
         def _(step):
-            m = (self.slot + step) % self.pairs
-            for kind in kinds:
-                self.paired(kind, step).wait_recv()
-                own = self.grads[kind][2 * m + self.parity].astype(F32)
-                self.acc[kind, m] = (own + self.recv1[kind, m].astype(F32)).astype(BF)
-                self.passed(kind, step).start()
-
-    def pair_only(self, kind, shares, own):
-        @pl.loop(1, self.pairs)
-        def _(step):
-            m = (self.slot + step) % self.pairs
-            self.paired(kind, step).wait_recv()
-            mine = self.grads[kind][2 * m + self.parity].astype(F32)
-            shares[m] = (mine + self.recv1[kind, m].astype(F32)).astype(BF)
-
-        self.paired(kind, self.pairs).wait_recv()
-        shares[self.slot] = jnp.zeros_like(shares[0])
-        own[...] = self.grads[kind][self.mine].astype(F32) + self.recv1[kind, self.slot].astype(F32)
-
-        @pl.loop(1, self.pairs + 1)
-        def _(step):
-            self.paired(kind, step).wait_send()
+            at = self.index(stage, step)
+            self.held[stage][kind, at] = self.total(kind, stage, self.given(stage, step)).astype(BF)
+            self.copy(kind, stage, step).start()
+
+    def rest(self, kind, first):
+        for stage in range(first, self.stages):
+            self.stage(kind, stage)
 
     def collect(self, kind):
-        self.paired(kind, self.pairs).wait_recv()
-        total = self.grads[kind][self.mine].astype(F32) + self.recv1[kind, self.slot].astype(F32)
-        for step in range(1, self.pairs):
-            self.passed(kind, step).wait_recv()
-            total += self.recv2[kind, (self.slot + self.pairs - step) % self.pairs].astype(F32)
-        return total
+        return self.total(kind, self.stages, self.mine)
 
     def end(self, kinds):
         for kind in kinds:
-            @pl.loop(1, self.pairs + 1)
-            def _(step):
-                self.paired(kind, step).wait_send()
-
-            @pl.loop(1, self.pairs)
-            def _(step):
-                self.passed(kind, step).wait_send()
+            for stage in range(self.stages):
+                @pl.loop(1, self.count(stage) + 1)
+                def _(step):
+                    self.copy(kind, stage, step).wait_send()
 
     @staticmethod
     def scratch(kinds, groups, held, span):
-        exchange = pltpu.VMEM((kinds, groups // 2, held, span), BF)
-        sems = pltpu.SemaphoreType.DMA((2, kinds, groups // 2 + 1))
-        return [exchange] * 3 + [sems] * 2
-
-
-class ShareSum:
-    def __init__(self, groups, shares, recv, sems):
-        self.shares, self.recv, self.sems = shares, recv, sems
-        self.pairs = groups // 2
-        mine = lax.axis_index("dp")
-        self.parity, self.slot = mine % 2, mine // 2
-
-    def passed(self, step):
-        m = (self.slot + step) % self.pairs
-        return send(self.shares.at[m], self.recv.at[self.slot], self.sems.at[0, step], self.sems.at[1, step],
-                    dp=2 * m + self.parity)
-
-    def start(self):
-        @pl.loop(1, self.pairs)
-        def _(step):
-            self.passed(step).start()
-
-    def collect(self, own):
-        total = own[...]
-        for step in range(1, self.pairs):
-            self.passed(step).wait()
-            total += self.recv[(self.slot + self.pairs - step) % self.pairs].astype(F32)
-        return total
+        stages = groups.bit_length() - 1
+        buffers = [pltpu.VMEM((kinds, groups >> (k + 1), held, span), BF) for k in range(stages)]
+        return buffers + buffers[1:] + [pltpu.SemaphoreType.DMA((2, kinds, stages, groups // 2 + 1))]
 
 
 class GiveBack:
@@ -556,11 +525,11 @@
 
 
 def mid_kernel(groups, blocks, grad_scale, context, packed, full_out, up_w, up_bias, down_w, cot_folded, v0, v1, v2, v3, v4, v5,
-               d_low, d_own, small, value_grad, down_grad, gate_shares, gate_sum, folded,
+               d_low, d_own, small, gate_grad, value_grad, down_grad, folded,
                normed_low, slope_term, gelu_term, gated, d_gate, d_value, unit_full, rs_full, unit_own, rs_own, d_mixed,
-               mixed, whole_grad, down_pieces, gate_pieces, cot_recv,
+               mixed, whole_grad, down_pieces, cot_recv,
                part1, first1, second1, third1, sems1, part2, first2, second2, third2, sems2, sems3, sems4, c_sems,
-               vector_rows, acc, recv1, recv2, pair_sems, group_sems):
+               vector_rows, *sum_scratch):
     me, sibling, across, diagonal = place_of()
     columns = packed.shape[1]
     width = columns // 4
@@ -578,7 +547,7 @@
     back_sum = RowSum(part2, first2, second2, third2, sems2)
     mixed_gather = RowGather(mixed, sems3)
     hidden_gather = RowGather(d_low, sems4)
-    sums = GroupSum(groups, (down_pieces, gate_pieces), (acc, recv1, recv2), (pair_sems, group_sems))
+    sums = GroupSum(groups, (down_pieces,), sum_scratch)
     small[...] = jnp.zeros_like(small)
     for k, vector in enumerate((v0, v1, v2, v3, v4, v5)):
         vector_rows[k : k + 1, :] = vector[...].astype(F32).reshape(1, columns)
@@ -700,19 +669,18 @@
     weight_grad(d_mixed_rows, gated, down_pieces)
     sums.start(0)
     finish(0)
-    weight_grad(normed_low[...], d_gate, gate_pieces)
-    sums.start(1)
+    weight_grad(normed_low[...], d_gate, gate_grad)
     if blocks > 1:
         finish(1)
     weight_grad(normed_low[...], d_value, value_grad)
     for b in range(2, blocks):
         finish(b)
+    sums.stage(0, 1)
     for b in range(blocks):
         hidden_gather.relay(b)
-    sums.forward((0,))
+    sums.rest(0, 2)
     for b in range(blocks):
         hidden_gather.land(b)
-    sums.pair_only(1, gate_shares, gate_sum)
     down_grad[...] = sums.collect(0)
     for b in range(blocks):
         mixed_gather.end(b)
@@ -736,8 +704,7 @@
         shape(own, F32),
         shape((16, columns), F32),
         shape((groups, held, units), BF),
-        shape((held, units), F32),
-        shape((groups // 2, held, units), BF),
+        shape((groups, held, units), BF),
         shape((held, units), F32),
         shape(cot_folded.shape, BF),
     )
@@ -760,24 +727,22 @@
             pltpu.VMEM((blocks, 4, quarter, columns), BF),
             pltpu.VMEM((columns, units), F32),
             pltpu.VMEM((groups, held, units), BF),
-            pltpu.VMEM((groups, held, units), BF),
             pltpu.VMEM(cot_folded.shape, BF),
         ]
         + RowSum.scratch(blocks, quarter, columns)
         + RowSum.scratch(blocks, quarter, columns)
         + [dma((6, blocks)), dma((6, blocks)), dma((2, 3)), pltpu.VMEM((6, columns), F32)]
-        + GroupSum.scratch(2, groups, held, units),
+        + GroupSum.scratch(1, groups, held, units),
         args,
     )
 
 
 def back_kernel(groups, blocks, grad_scale, dh_low, dh_own, qkv, lse, seq_row, context, packed_in, qkv_w,
-                out_w, value_grad, gate_shares, gate_sum, folded, small, taking,
-                layer_out, input_grad, up_grad, qkv_grad, out_grad, small_out,
+                out_w, gate_grad, value_grad, folded, small, taking,
+                layer_out, input_grad, up_grad, qkv_grad, out_grad, small_out, qv_out, up_out,
                 d_rows, d_part, late_sum, late, cols, one, two, three, packed, ssent, srecv, swide, x_sems, s_sems, w_sems,
                 start_col, chosen, weight_here, returned, landed, load_sem, r_sems,
-                acc, recv1, recv2, pair_sems, group_sems, acc2, recv3, recv4, pair_sems2, group_sems2, share_recv, share_sems,
-                sent, recv, a_sems, sent2, recv5, a_sems2):
+                sent, recv, a_sems, sent2, recv5, a_sems2, *sum_scratch):
     me, sibling, across, diagonal = place_of()
     mine = lax.axis_index("dp")
     width, rows = input_grad.shape
@@ -789,13 +754,13 @@
     load_rows = pltpu.make_async_copy(taking, chosen, load_sem.at[1])
     load_rows.start()
     enter([sibling, across, diagonal], groups)
-    sums = GroupSum(groups, (value_grad,), (acc, recv1, recv2), (pair_sems, group_sems))
-    late_sums = GroupSum(groups, (late,), (acc2, recv3, recv4), (pair_sems2, group_sems2))
+    half_scratch = len(sum_scratch) // 2
+    sums = GroupSum(groups, (gate_grad, value_grad), sum_scratch[:half_scratch])
+    late_sums = GroupSum(groups, (late,), sum_scratch[half_scratch:])
     giving = GiveBack(groups, rows, width, chosen, sent, recv, a_sems)
     giving_result = GiveBack(groups, rows, width, chosen, sent2, recv5, a_sems2)
-    gate = ShareSum(groups, gate_shares, share_recv, share_sems)
-    gate.start()
     sums.start(0)
+    sums.start(1)
     returns = [
         send(folded.at[peer], returned.at[me], r_sems.at[0, k], r_sems.at[1, k], tensor=peer)
         for k, peer in enumerate((across, diagonal, sibling))
@@ -861,7 +826,7 @@
 
         @pl.when(b == 0)
         def _():
-            sums.forward((0,))
+            sums.stage(0, 1)
 
         @pl.when(b == 1)
         def _():
@@ -872,7 +837,12 @@
                 for s in range(4):
                     start = q * BLOCK + s * quarter
                     packed[start : start + quarter, :] = unfold(returned[s, q], width, True)
+            sums.rest(0, 2)
             giving_result.start(packed)
+
+        @pl.when(b == 2)
+        def _():
+            sums.stage(1, 1)
 
     for c in range(3):
         late_sum[:, c * width : (c + 1) * width] = dot(packed_in[...], d_rows[c], ((0,), (0,)))
@@ -880,6 +850,7 @@
         late[g] = (late_sum[g * held : (g + 1) * held, :] * grad_scale).astype(BF)
 
     late_sums.start(0)
+    sums.rest(1, 2)
     swaps = [
         send(ssent, srecv.at[me], s_sems.at[0, k], s_sems.at[1, k], tensor=peer)
         for k, peer in enumerate((sibling, across, diagonal))
@@ -909,9 +880,9 @@
     def _(step):
         spread(step).start()
 
-    late_sums.forward((0,))
-    up_grad[0] = gate.collect(gate_sum)
-    up_grad[1] = sums.collect(0)
+    late_sums.rest(0, 1)
+    up_grad[0] = sums.collect(0)
+    up_grad[1] = sums.collect(1)
     giving_result.land(landed)
     layer_out[...] = landed[...].T
 
@@ -919,12 +890,18 @@
     def _(step):
         spread(step).wait_recv()
 
-    small_out[...] = swide[0]
+    for swap in swaps:
+        swap.wait_send()
+    ssent[...] = swide[0]
 
     @pl.loop(1, groups)
     def _(peer):
-        small_out[...] += swide[peer]
-
+        ssent[...] += swide[peer]
+
+    small_out[...] = ssent[0:8, :]
+    up_out[...] = ssent[8:10, :]
+    for k in range(2):
+        qv_out[k : k + 1, :] = ssent[10:11, k * 256 : k * 256 + width]
     total = late_sums.collect(0)
     for c in range(3):
         qkv_grad[c] = total[:, c * width : (c + 1) * width]
@@ -933,9 +910,9 @@
     input_grad[...] = landed[...].T
     for b in range(blocks):
         far(b).wait_send()
-    for copy in swaps + returns:
+    for copy in returns:
         copy.wait_send()
-    sums.end((0,))
+    sums.end((0, 1))
     late_sums.end((0,))
 
     @pl.loop(1, groups)
@@ -944,7 +921,7 @@
 
 
 def back(groups, grad_scale, args, small, number):
-    dh_low, qkv, qkv_w, grad, folded = args[0], args[2], args[7], args[9], args[12]
+    dh_low, qkv, qkv_w, grad, folded = args[0], args[2], args[7], args[9], args[11]
     rows, columns = dh_low.shape
     width = qkv.shape[2]
     held, units = grad.shape[1:]
@@ -957,7 +934,9 @@
         shape((2, held, units), F32),
         shape((3, held, width), F32),
         shape((width, held), F32),
-        shape(small.shape, F32),
+        shape((8, columns), F32),
+        shape((2, width), F32),
+        shape((2, units), F32),
     )
     return call(
         functools.partial(back_kernel, groups, blocks, grad_scale),
@@ -987,13 +966,12 @@
             dma((2,)),
             dma((2, 3)),
         ]
-        + GroupSum.scratch(1, groups, held, units)
-        + GroupSum.scratch(1, groups, held, 4 * width)
-        + [pltpu.VMEM((groups // 2, held, units), BF), dma((2, groups // 2))]
         + GiveBack.scratch(groups, rows, width)
-        + GiveBack.scratch(groups, rows, width),
+        + GiveBack.scratch(groups, rows, width)
+        + GroupSum.scratch(2, groups, held, units)
+        + GroupSum.scratch(1, groups, held, 4 * width),
         args,
-        apart=(7, 14),
+        apart=(7, 13),
     )
 
 
@@ -1024,7 +1002,7 @@
     packed_in, cot_folded, full_out, qkv_rows, log_total, context, wide_context, taking = front(
         groups, (tokens.T, cotangent.T, row_place, seq_row, weight_turned, qv_bias, out_weight), 0
     )
-    d_low, d_own, small, value_grad, down_grad, gate_shares, gate_sum, folded = mid(
+    d_low, d_own, small, gate_grad, value_grad, down_grad, folded = mid(
         groups,
         grad_scale,
         (
@@ -1044,7 +1022,7 @@
         ),
         1,
     )
-    layer_out, input_grad, up_grad, qkv_grad, out_grad, sums = back(
+    layer_out, input_grad, up_grad, qkv_grad, out_grad, sums, qv_bias_grad, up_bias_grad = back(
         groups,
         grad_scale,
         (
@@ -1057,9 +1035,8 @@
             packed_in,
             weight_turned,
             out_weight,
+            gate_grad,
             value_grad,
-            gate_shares,
-            gate_sum,
             folded,
             small,
             taking,
@@ -1073,13 +1050,13 @@
         layer_out.T,
         input_grad.T,
         qkv_grad,
-        jnp.stack([sums[10, :width], sums[10, 256 : 256 + width]]),
+        qv_bias_grad,
         out_grad,
         sums_here[0],
         sums_here[1],
         sums_here[2],
         up_grad,
-        sums[8:10],
+        up_bias_grad,
         down_grad.T,
         sums_here[3],
         sums_here[4],

time: 250 us -> 245 us (0.980)
  Pallas kernels: 233 us -> 230 us
    slice x3 -> x0, local copies, waits for them, and re-layouts: 2.88 us -> none  [the longest x1 1.33 us: on_device(): sums[8:10]]
    pallas_call x3, Pallas kernels: 233 us -> 230 us  [call(): pl.pallas_call(kernel, out_shape=outs, in_specs=specs, out_specs=tuple((p...]
    unnamed x14 -> x20, local copies, waits for them, and re-layouts: 6.73 us -> 7.91 us
where the time goes in v1:
time: 245 us; the launch traced here: 242 us
  Pallas kernels  230 us (94%)
  local copies, waits for them, and re-layouts  10.6 us (4%)
    pallas_call x3, Pallas kernels, call(): pl.pallas_call(kernel, out_shape=outs, in_specs=specs, out_specs=tuple((p...  230 us
    unnamed x20, local copies, waits for them, and re-layouts  7.91 us

profile of v1, /device:TPU:0, one launch (start us, length us, event | category | flops | bytes accessed | tf_op | source)
XLA Modules:
  0.0 241.7 jit_solution(14531050040227770037)
XLA Ops:
  0.6 1.3 reshape.37.seq_row
  1.9 55.8 %shard_map.263 = (bf16[1536,768]{1,0:T(8,128)(2,1)}, bf16[4,3,64,384]{3,2,1,0:T(8,128)(2,1)}, bf16[4,192,768]{2,1,0:T(8,128)(2,1)}, bf16[3,1536,192]{2,1,0:T(8,1...) custom-call(bf16[192,1536]{1,0:T(8,128)(2,1)} %bitcast.27, ...), custom_call_target="tpu_custom_call" | custom-call | tf_op jit(solution)/shard_map/pallas_call | solution.py:73
  57.7 90.6 %shard_map.264 = (bf16[3,4,128,768]{3,2,1,0:T(8,128)(2,1)}, f32[3,128,768]{2,1,0:T(8,128)}, f32[16,768]{1,0:T(8,128)}, bf16[8,96,768]{2,1,0:T(8,128)(2,1)}, bf16...) custom-call(bf16[1536,768]{1,0:T(8,128)(2,1)} %get-tuple-element.37.context, ...), custom_call_target="tpu_custom_call" | custom-call | tf_op jit(solution)/shard_map/pallas_call | solution.py:73
  148.3 83.8 %shard_map.265 = (bf16[192,1536]{1,0:T(8,128)(2,1)}, bf16[192,1536]{1,0:T(8,128)(2,1)}, f32[2,96,768]{2,1,0:T(8,128)}, f32[3,96,192]{2,1,0:T(8,128)}, f32[192,96...) custom-call(bf16[1536,768]{1,0:T(8,128)(2,1)} %bitcast.23, ...), custom_call_target="tpu_custom_call" | custom-call | tf_op jit(solution)/shard_map/pallas_call | solution.py:73
  232.1 0.0 copy-start.2
  232.1 0.0 copy-start.5
  232.2 0.0 copy-start.3
  232.2 0.0 copy-start
  232.2 0.0 copy-start.4
  232.2 0.0 copy-start.1
  232.2 0.9 constant_dynamic-slice_fusion
  233.1 0.5 slice_bitcast_fusion
  233.6 1.9 copy.38
  235.5 1.9 copy.39
  237.4 0.0 copy-done.2
  237.4 0.7 copy.40
  238.2 0.0 copy-done.5
  238.2 0.6 copy.41
  238.7 0.0 copy-done.3
  238.7 0.6 copy.42
  239.4 0.0 copy-done
  239.4 0.8 copy.43
  240.2 0.0 copy-done.4
  240.2 0.6 copy.44
  240.8 0.0 copy-done.1
  240.8 0.7 copy.45
Async XLA Ops:
  232.1 5.3 %copy-start.2 = (f32[3,96,192]{2,1,0:T(8,128)S(1)}, f32[3,96,192]{2,1,0:T(8,128)}, u32[]{:S(2)}) copy-start(f32[3,96,192]{2,1,0:T(8,128)} %get-tuple-element.82) | copy-start | bytes 663556
  232.1 6.0 %copy-start.5 = (f32[2,192]{1,0:T(2,128)S(1)}, f32[2,192]{1,0:T(2,128)}, u32[]{:S(2)}) copy-start(f32[2,192]{1,0:T(2,128)} %get-tuple-element.83) | copy-start | bytes 4612
  232.2 6.6 %copy-start.3 = (f32[192,96]{1,0:T(8,128)S(1)}, f32[192,96]{1,0:T(8,128)}, u32[]{:S(2)}) copy-start(f32[192,96]{1,0:T(8,128)} %get-tuple-element.84) | copy-start | bytes 221188
  232.2 7.2 %copy-start = (f32[2,96,768]{2,1,0:T(8,128)S(1)}, f32[2,96,768]{2,1,0:T(8,128)}, u32[]{:S(2)}) copy-start(f32[2,96,768]{2,1,0:T(8,128)} %get-tuple-element.88) | copy-start | bytes 1769476
  232.2 8.0 %copy-start.4 = (f32[2,768]{1,0:T(2,128)S(1)}, f32[2,768]{1,0:T(2,128)}, u32[]{:S(2)}) copy-start(f32[2,768]{1,0:T(2,128)} %get-tuple-element.89) | copy-start | bytes 18436
  232.2 8.6 %copy-start.1 = (f32[96,768]{1,0:T(8,128)S(1)}, f32[96,768]{1,0:T(8,128)}, u32[]{:S(2)}) copy-start(f32[96,768]{1,0:T(8,128)} %get-tuple-element.59) | copy-start | bytes 884740

commit v2 on v1

--- a/solution.py
+++ b/solution.py
@@ -187,7 +187,6 @@
     out_near.start()
     loads[1].wait()
     cot_here[...] = cot_turned[...].T
-    give(1, cot_here)
     full_out[me] = out_w[...]
     to_column(seq_row, start_col, 0)
     for b in range(blocks):
@@ -224,6 +223,7 @@
         token_gather.start(b, placed(b))
         if b >= 1:
             token_gather.relay(b - 1)
+    give(1, cot_here)
     loads[2].wait()
 
     def attend(b):
@@ -339,13 +339,18 @@
 
 
 class GroupSum:
-    def __init__(self, groups, grads, scratch):
-        self.groups, self.grads = groups, grads
+    def __init__(self, groups, grads, scratch, turned):
+        self.groups, self.grads, self.turned = groups, grads, turned
         self.stages = groups.bit_length() - 1
         self.recv = scratch[: self.stages]
         self.held = (None,) + tuple(scratch[self.stages : 2 * self.stages - 1])
         self.sems = scratch[-1]
-        self.mine = lax.axis_index("dp")
+        mine = lax.axis_index("dp")
+        self.mine = mine // 2 + mine % 2 * (groups // 2) if turned else mine
+
+    def real(self, device):
+        half = self.groups // 2
+        return device % half * 2 + device // half if self.turned else device
 
     def count(self, stage):
         return self.groups >> (stage + 1)
@@ -358,55 +363,61 @@
         low = self.mine % (1 << stage)
         return self.index(stage, step) * (2 << stage) + (1 - bit) * (1 << stage) + low
 
-    def copy(self, kind, stage, step):
+    def copy(self, stage, step):
         bit = (self.mine // (1 << stage)) % 2
         partner = self.mine + (1 - 2 * bit) * (1 << stage)
         at = self.index(stage, step)
-        source = self.held[stage].at[kind, at] if stage else self.grads[kind].at[self.given(0, step)]
-        return send(source, self.recv[stage].at[kind, at], self.sems.at[0, kind, stage, step],
-                    self.sems.at[1, kind, stage, step], dp=partner)
-
-    def start(self, kind):
+        source = self.held[stage].at[at] if stage else self.grads.at[self.real(self.given(0, step))]
+        return send(source, self.recv[stage].at[at], self.sems.at[0, stage, step], self.sems.at[1, stage, step],
+                    dp=self.real(partner))
+
+    def start(self):
         @pl.loop(1, self.count(0) + 1)
         def _(step):
-            self.copy(kind, 0, step).start()
-
-    def total(self, kind, stages, piece):
-        total = self.grads[kind][piece].astype(F32)
+            self.copy(0, step).start()
+
+    def total(self, stages, piece):
+        total = self.grads[self.real(piece)].astype(F32)
         for stage in range(stages):
             count = self.count(stage)
             at = piece // (2 << stage)
             step = (at + 2 * count - 1 - self.mine // (2 << stage)) % count + 1
-            self.copy(kind, stage, step).wait_recv()
-            total += self.recv[stage][kind, at].astype(F32)
+            self.copy(stage, step).wait_recv()
+            total += self.recv[stage][at].astype(F32)
         return total
 
-    def stage(self, kind, stage):
+    def stage(self, stage):
         @pl.loop(1, self.count(stage) + 1)
         def _(step):
             at = self.index(stage, step)
-            self.held[stage][kind, at] = self.total(kind, stage, self.given(stage, step)).astype(BF)
-            self.copy(kind, stage, step).start()
-
-    def rest(self, kind, first):
+            self.held[stage][at] = self.total(stage, self.given(stage, step)).astype(BF)
+            self.copy(stage, step).start()
+
+    def rest(self, first):
         for stage in range(first, self.stages):
-            self.stage(kind, stage)
-
-    def collect(self, kind):
-        return self.total(kind, self.stages, self.mine)
-
-    def end(self, kinds):
-        for kind in kinds:
-            for stage in range(self.stages):
-                @pl.loop(1, self.count(stage) + 1)
-                def _(step):
-                    self.copy(kind, stage, step).wait_send()
+            self.stage(stage)
+
+    def collect(self):
+        return self.total(self.stages, self.mine)
+
+    def end(self):
+        for stage in range(self.stages):
+            @pl.loop(1, self.count(stage) + 1)
+            def _(step):
+                self.copy(stage, step).wait_send()
 
     @staticmethod
-    def scratch(kinds, groups, held, span):
+    def scratch(groups, held, span):
         stages = groups.bit_length() - 1
-        buffers = [pltpu.VMEM((kinds, groups >> (k + 1), held, span), BF) for k in range(stages)]
-        return buffers + buffers[1:] + [pltpu.SemaphoreType.DMA((2, kinds, stages, groups // 2 + 1))]
+        buffers = [pltpu.VMEM((groups >> (k + 1), held, span), BF) for k in range(stages)]
+        return buffers + buffers[1:] + [pltpu.SemaphoreType.DMA((2, stages, groups // 2 + 1))]
+
+
+def both_ways(groups, pair, scratch):
+    half = len(scratch) // 2
+    return [
+        GroupSum(groups, grads, scratch[k * half : (k + 1) * half], k == 1) for k, grads in enumerate(pair)
+    ]
 
 
 class GiveBack:
@@ -527,14 +538,14 @@
 def mid_kernel(groups, blocks, grad_scale, context, packed, full_out, up_w, up_bias, down_w, cot_folded, v0, v1, v2, v3, v4, v5,
                d_low, d_own, small, gate_grad, value_grad, down_grad, folded,
                normed_low, slope_term, gelu_term, gated, d_gate, d_value, unit_full, rs_full, unit_own, rs_own, d_mixed,
-               mixed, whole_grad, down_pieces, cot_recv,
+               mixed, whole_grad, down_left, down_right, cot_recv,
                part1, first1, second1, third1, sems1, part2, first2, second2, third2, sems2, sems3, sems4, c_sems,
                vector_rows, *sum_scratch):
     me, sibling, across, diagonal = place_of()
     columns = packed.shape[1]
     width = columns // 4
     quarter = BLOCK // 4
-    held = down_pieces.shape[1]
+    held = down_left.shape[1]
     enter([sibling, across, diagonal], groups)
     swaps = [
         send(cot_folded.at[peer], cot_recv.at[me], c_sems.at[0, k], c_sems.at[1, k], tensor=peer)
@@ -547,7 +558,7 @@
     back_sum = RowSum(part2, first2, second2, third2, sems2)
     mixed_gather = RowGather(mixed, sems3)
     hidden_gather = RowGather(d_low, sems4)
-    sums = GroupSum(groups, (down_pieces,), sum_scratch)
+    sums = both_ways(groups, (down_left, down_right), sum_scratch)
     small[...] = jnp.zeros_like(small)
     for k, vector in enumerate((v0, v1, v2, v3, v4, v5)):
         vector_rows[k : k + 1, :] = vector[...].astype(F32).reshape(1, columns)
@@ -639,7 +650,9 @@
             lanes = slice(c * CHUNK, (c + 1) * CHUNK)
             whole_grad[:, lanes] = dot(left, right[:, lanes], ((0,), (0,)))
         for g in range(groups):
-            pieces[g] = (whole_grad[g * held : (g + 1) * held, :] * grad_scale).astype(BF)
+            rows_here = (whole_grad[g * held : (g + 1) * held, :] * grad_scale).astype(BF)
+            for k, target in enumerate(pieces):
+                target[g] = rows_here[:, k * target.shape[2] : (k + 1) * target.shape[2]]
 
     last = blocks - 1
     for b in range(blocks):
@@ -666,28 +679,34 @@
             back_sum.relay(b - 1)
     back_sum.relay(last)
     d_mixed_rows = jnp.concatenate([mixed[b, k] for b in range(blocks) for k in range(4)], axis=0)
-    weight_grad(d_mixed_rows, gated, down_pieces)
-    sums.start(0)
+    weight_grad(d_mixed_rows, gated, (down_left, down_right))
+    for half in sums:
+        half.start()
     finish(0)
-    weight_grad(normed_low[...], d_gate, gate_grad)
+    weight_grad(normed_low[...], d_gate, (gate_grad,))
     if blocks > 1:
         finish(1)
-    weight_grad(normed_low[...], d_value, value_grad)
+    weight_grad(normed_low[...], d_value, (value_grad,))
     for b in range(2, blocks):
         finish(b)
-    sums.stage(0, 1)
+    for half in sums:
+        half.stage(1)
     for b in range(blocks):
         hidden_gather.relay(b)
-    sums.rest(0, 2)
+    for half in sums:
+        half.rest(2)
     for b in range(blocks):
         hidden_gather.land(b)
-    down_grad[...] = sums.collect(0)
+    for k, half in enumerate(sums):
+        span = half.grads.shape[2]
+        down_grad[:, k * span : (k + 1) * span] = half.collect()
     for b in range(blocks):
         mixed_gather.end(b)
         hidden_gather.end(b)
     for swap in swaps:
         swap.wait_send()
-    sums.end((0,))
+    for half in sums:
+        half.end()
 
 
 def mid(groups, grad_scale, args, number):
@@ -726,13 +745,15 @@
             pltpu.VMEM(own, F32),
             pltpu.VMEM((blocks, 4, quarter, columns), BF),
             pltpu.VMEM((columns, units), F32),
-            pltpu.VMEM((groups, held, units), BF),
+            pltpu.VMEM((groups, held, units // 2), BF),
+            pltpu.VMEM((groups, held, units // 2), BF),
             pltpu.VMEM(cot_folded.shape, BF),
         ]
         + RowSum.scratch(blocks, quarter, columns)
         + RowSum.scratch(blocks, quarter, columns)
         + [dma((6, blocks)), dma((6, blocks)), dma((2, 3)), pltpu.VMEM((6, columns), F32)]
-        + GroupSum.scratch(1, groups, held, units),
+        + GroupSum.scratch(groups, held, units // 2)
+        + GroupSum.scratch(groups, held, units // 2),
         args,
     )
 
@@ -740,14 +761,14 @@
 def back_kernel(groups, blocks, grad_scale, dh_low, dh_own, qkv, lse, seq_row, context, packed_in, qkv_w,
                 out_w, gate_grad, value_grad, folded, small, taking,
                 layer_out, input_grad, up_grad, qkv_grad, out_grad, small_out, qv_out, up_out,
-                d_rows, d_part, late_sum, late, cols, one, two, three, packed, ssent, srecv, swide, x_sems, s_sems, w_sems,
+                d_rows, d_part, late_sum, late_left, late_right, cols, one, two, three, packed, ssent, srecv, swide, x_sems, s_sems, w_sems,
                 start_col, chosen, weight_here, returned, landed, load_sem, r_sems,
                 sent, recv, a_sems, sent2, recv5, a_sems2, *sum_scratch):
     me, sibling, across, diagonal = place_of()
     mine = lax.axis_index("dp")
     width, rows = input_grad.shape
     heads = width // HEAD_DIM
-    held = late.shape[1]
+    held = late_left.shape[1]
     quarter = BLOCK // 4
     load = pltpu.make_async_copy(qkv_w, weight_here, load_sem.at[0])
     load.start()
@@ -755,12 +776,12 @@
     load_rows.start()
     enter([sibling, across, diagonal], groups)
     half_scratch = len(sum_scratch) // 2
-    sums = GroupSum(groups, (gate_grad, value_grad), sum_scratch[:half_scratch])
-    late_sums = GroupSum(groups, (late,), sum_scratch[half_scratch:])
+    sums = both_ways(groups, (gate_grad, value_grad), sum_scratch[:half_scratch])
+    late_sums = both_ways(groups, (late_left, late_right), sum_scratch[half_scratch:])
     giving = GiveBack(groups, rows, width, chosen, sent, recv, a_sems)
     giving_result = GiveBack(groups, rows, width, chosen, sent2, recv5, a_sems2)
-    sums.start(0)
-    sums.start(1)
+    for each in sums:
+        each.start()
     returns = [
         send(folded.at[peer], returned.at[me], r_sems.at[0, k], r_sems.at[1, k], tensor=peer)
         for k, peer in enumerate((across, diagonal, sibling))
@@ -826,7 +847,8 @@
 
         @pl.when(b == 0)
         def _():
-            sums.stage(0, 1)
+            for each in sums:
+                each.stage(1)
 
         @pl.when(b == 1)
         def _():
@@ -837,20 +859,19 @@
                 for s in range(4):
                     start = q * BLOCK + s * quarter
                     packed[start : start + quarter, :] = unfold(returned[s, q], width, True)
-            sums.rest(0, 2)
+            for each in sums:
+                each.rest(2)
             giving_result.start(packed)
-
-        @pl.when(b == 2)
-        def _():
-            sums.stage(1, 1)
 
     for c in range(3):
         late_sum[:, c * width : (c + 1) * width] = dot(packed_in[...], d_rows[c], ((0,), (0,)))
     for g in range(groups):
-        late[g] = (late_sum[g * held : (g + 1) * held, :] * grad_scale).astype(BF)
-
-    late_sums.start(0)
-    sums.rest(1, 2)
+        rows_here = (late_sum[g * held : (g + 1) * held, :] * grad_scale).astype(BF)
+        late_left[g] = rows_here[:, : 2 * width]
+        late_right[g] = rows_here[:, 2 * width :]
+
+    for each in late_sums:
+        each.start()
     swaps = [
         send(ssent, srecv.at[me], s_sems.at[0, k], s_sems.at[1, k], tensor=peer)
         for k, peer in enumerate((sibling, across, diagonal))
@@ -880,9 +901,11 @@
     def _(step):
         spread(step).start()
 
-    late_sums.rest(0, 1)
-    up_grad[0] = sums.collect(0)
-    up_grad[1] = sums.collect(1)
+    for stage in range(1, late_sums[0].stages):
+        for each in late_sums:
+            each.stage(stage)
+    for k, each in enumerate(sums):
+        up_grad[k] = each.collect()
     giving_result.land(landed)
     layer_out[...] = landed[...].T
 
@@ -902,18 +925,21 @@
     up_out[...] = ssent[8:10, :]
     for k in range(2):
         qv_out[k : k + 1, :] = ssent[10:11, k * 256 : k * 256 + width]
-    total = late_sums.collect(0)
-    for c in range(3):
-        qkv_grad[c] = total[:, c * width : (c + 1) * width]
-    out_grad[...] = total[:, 3 * width :].T
+    for k, each in enumerate(late_sums):
+        total = each.collect()
+        qkv_grad[2 * k] = total[:, :width]
+        if k == 0:
+            qkv_grad[1] = total[:, width:]
+        else:
+            out_grad[...] = total[:, width:].T
     giving.land(landed)
     input_grad[...] = landed[...].T
     for b in range(blocks):
         far(b).wait_send()
     for copy in returns:
         copy.wait_send()
-    sums.end((0, 1))
-    late_sums.end((0,))
+    for each in sums + late_sums:
+        each.end()
 
     @pl.loop(1, groups)
     def _(step):
@@ -946,7 +972,8 @@
             pltpu.VMEM((3, rows, width), BF),
             pltpu.VMEM((BLOCK, columns), F32),
             pltpu.VMEM((columns, 4 * width), F32),
-            pltpu.VMEM((groups, held, 4 * width), BF),
+            pltpu.VMEM((groups, held, 2 * width), BF),
+            pltpu.VMEM((groups, held, 2 * width), BF),
             pltpu.VMEM((4,) + half, BF),
             pltpu.VMEM(half, BF),
             pltpu.VMEM(half, BF),
@@ -968,8 +995,8 @@
         ]
         + GiveBack.scratch(groups, rows, width)
         + GiveBack.scratch(groups, rows, width)
-        + GroupSum.scratch(2, groups, held, units)
-        + GroupSum.scratch(1, groups, held, 4 * width),
+        + GroupSum.scratch(groups, held, units) * 2
+        + GroupSum.scratch(groups, held, 2 * width) * 2,
         args,
         apart=(7, 13),
     )

time: 245 us -> 242 us (0.988)
  Pallas kernels: 230 us -> 227 us
    pallas_call x3, Pallas kernels: 230 us -> 227 us  [call(): pl.pallas_call(kernel, out_shape=outs, in_specs=specs, out_specs=tuple((p...]
where the time goes in v2:
time: 242 us; the launch traced here: 238 us
  Pallas kernels  227 us (94%)
  local copies, waits for them, and re-layouts  10.6 us (4%)
    pallas_call x3, Pallas kernels, call(): pl.pallas_call(kernel, out_shape=outs, in_specs=specs, out_specs=tuple((p...  227 us
    unnamed x20, local copies, waits for them, and re-layouts  7.91 us

profile of v2, /device:TPU:0, one launch (start us, length us, event | category | flops | bytes accessed | tf_op | source)
XLA Modules:
  0.0 238.3 jit_solution(13135278263436264085)
XLA Ops:
  0.6 1.3 reshape.37.seq_row
  1.9 56.2 %shard_map.263 = (bf16[1536,768]{1,0:T(8,128)(2,1)}, bf16[4,3,64,384]{3,2,1,0:T(8,128)(2,1)}, bf16[4,192,768]{2,1,0:T(8,128)(2,1)}, bf16[3,1536,192]{2,1,0:T(8,1...) custom-call(bf16[192,1536]{1,0:T(8,128)(2,1)} %bitcast.27, ...), custom_call_target="tpu_custom_call" | custom-call | tf_op jit(solution)/shard_map/pallas_call | solution.py:73
  58.1 81.8 %shard_map.264 = (bf16[3,4,128,768]{3,2,1,0:T(8,128)(2,1)}, f32[3,128,768]{2,1,0:T(8,128)}, f32[16,768]{1,0:T(8,128)}, bf16[8,96,768]{2,1,0:T(8,128)(2,1)}, bf16...) custom-call(bf16[1536,768]{1,0:T(8,128)(2,1)} %get-tuple-element.37.context, ...), custom_call_target="tpu_custom_call" | custom-call | tf_op jit(solution)/shard_map/pallas_call | solution.py:73
  140.0 88.5 %shard_map.265 = (bf16[192,1536]{1,0:T(8,128)(2,1)}, bf16[192,1536]{1,0:T(8,128)(2,1)}, f32[2,96,768]{2,1,0:T(8,128)}, f32[3,96,192]{2,1,0:T(8,128)}, f32[192,96...) custom-call(bf16[1536,768]{1,0:T(8,128)(2,1)} %bitcast.23, ...), custom_call_target="tpu_custom_call" | custom-call | tf_op jit(solution)/shard_map/pallas_call | solution.py:73
  228.5 0.0 copy-start.2
  228.5 0.0 copy-start.5
  228.5 0.0 copy-start.3
  228.5 0.0 copy-start
  228.5 0.0 copy-start.4
  228.5 0.0 copy-start.1
  228.5 0.9 constant_dynamic-slice_fusion
  229.4 0.5 slice_bitcast_fusion
  229.9 1.9 copy.38
  231.8 1.9 copy.39
  233.8 0.0 copy-done.2
  233.8 0.7 copy.40
  234.5 0.0 copy-done.5
  234.5 0.6 copy.41
  235.1 0.0 copy-done.3
  235.1 0.6 copy.42
  235.7 0.0 copy-done
  235.7 0.8 copy.43
  236.5 0.0 copy-done.4
  236.5 0.6 copy.44
  237.1 0.0 copy-done.1
  237.1 0.7 copy.45
Async XLA Ops:
  228.5 5.3 %copy-start.2 = (f32[3,96,192]{2,1,0:T(8,128)S(1)}, f32[3,96,192]{2,1,0:T(8,128)}, u32[]{:S(2)}) copy-start(f32[3,96,192]{2,1,0:T(8,128)} %get-tuple-element.82) | copy-start | bytes 663556
  228.5 6.0 %copy-start.5 = (f32[2,192]{1,0:T(2,128)S(1)}, f32[2,192]{1,0:T(2,128)}, u32[]{:S(2)}) copy-start(f32[2,192]{1,0:T(2,128)} %get-tuple-element.83) | copy-start | bytes 4612
  228.5 6.6 %copy-start.3 = (f32[192,96]{1,0:T(8,128)S(1)}, f32[192,96]{1,0:T(8,128)}, u32[]{:S(2)}) copy-start(f32[192,96]{1,0:T(8,128)} %get-tuple-element.84) | copy-start | bytes 221188
  228.5 7.2 %copy-start = (f32[2,96,768]{2,1,0:T(8,128)S(1)}, f32[2,96,768]{2,1,0:T(8,128)}, u32[]{:S(2)}) copy-start(f32[2,96,768]{2,1,0:T(8,128)} %get-tuple-element.88) | copy-start | bytes 1769476
  228.5 8.0 %copy-start.4 = (f32[2,768]{1,0:T(2,128)S(1)}, f32[2,768]{1,0:T(2,128)}, u32[]{:S(2)}) copy-start(f32[2,768]{1,0:T(2,128)} %get-tuple-element.89) | copy-start | bytes 18436
  228.5 8.6 %copy-start.1 = (f32[96,768]{1,0:T(8,128)S(1)}, f32[96,768]{1,0:T(8,128)}, u32[]{:S(2)}) copy-start(f32[96,768]{1,0:T(8,128)} %get-tuple-element.59) | copy-start | bytes 884740

commit v3 on v2

--- a/solution.py
+++ b/solution.py
@@ -413,10 +413,10 @@
         return buffers + buffers[1:] + [pltpu.SemaphoreType.DMA((2, stages, groups // 2 + 1))]
 
 
-def both_ways(groups, pair, scratch):
+def both_ways(groups, pair, scratch, turned=True):
     half = len(scratch) // 2
     return [
-        GroupSum(groups, grads, scratch[k * half : (k + 1) * half], k == 1) for k, grads in enumerate(pair)
+        GroupSum(groups, grads, scratch[k * half : (k + 1) * half], turned and k == 1) for k, grads in enumerate(pair)
     ]
 
 
@@ -776,7 +776,7 @@
     load_rows.start()
     enter([sibling, across, diagonal], groups)
     half_scratch = len(sum_scratch) // 2
-    sums = both_ways(groups, (gate_grad, value_grad), sum_scratch[:half_scratch])
+    sums = both_ways(groups, (gate_grad, value_grad), sum_scratch[:half_scratch], False)
     late_sums = both_ways(groups, (late_left, late_right), sum_scratch[half_scratch:])
     giving = GiveBack(groups, rows, width, chosen, sent, recv, a_sems)
     giving_result = GiveBack(groups, rows, width, chosen, sent2, recv5, a_sems2)
@@ -830,6 +830,36 @@
             d_rows[1, here, lanes] = (dot(d_scores, queries, ((1,), (0,))) * (HEAD_DIM**-0.5)).astype(BF)
             turned = dot(keys.T, d_scores, ((1,), (0,))) * (HEAD_DIM**-0.5)
             d_rows[0, here, lanes] = turned.T.astype(BF)
+        last = small.shape[0] - 6
+        for k, c in enumerate((0, 2)):
+            bias = jnp.sum(d_rows[c, here, :].astype(F32), axis=0, keepdims=True) * grad_scale
+            ssent[last : last + 1, k * 2 * 128 : k * 2 * 128 + width] += bias
+        @pl.when(b == 1)
+        def _():
+            load_rows.wait()
+            for swap in returns:
+                swap.wait_recv()
+            for q in range(blocks):
+                for s in range(4):
+                    start = q * BLOCK + s * quarter
+                    packed[start : start + quarter, :] = unfold(returned[s, q], width, True)
+            giving_result.start(packed)
+            sums[0].stage(1)
+
+    for c in range(3):
+        late_sum[:, c * width : (c + 1) * width] = dot(packed_in[...], d_rows[c], ((0,), (0,)))
+    for g in range(groups):
+        rows_here = (late_sum[g * held : (g + 1) * held, :] * grad_scale).astype(BF)
+        late_left[g] = rows_here[:, : 2 * width]
+        late_right[g] = rows_here[:, 2 * width :]
+
+    for each in late_sums:
+        each.start()
+    sums[0].rest(2)
+
+    @pl.loop(0, blocks)
+    def _(b):
+        here = pl.ds(pl.multiple_of(b * BLOCK, BLOCK), BLOCK)
         part = dot(d_rows[0, here, :], weight_here[0], ((1,), (0,)))
         part += dot(d_rows[1, here, :], weight_here[1], ((1,), (0,)))
         part += dot(d_rows[2, here, :], weight_here[2], ((1,), (0,)))
@@ -839,39 +869,9 @@
             fold_into(cols, (u, b), d_part[:, u * width : (u + 1) * width].astype(BF), True)
         cross(b).start()
         near(b).start()
-        last = small.shape[0] - 6
-        for k, c in enumerate((0, 2)):
-            bias = jnp.sum(d_rows[c, here, :].astype(F32), axis=0, keepdims=True) * grad_scale
-            ssent[last : last + 1, k * 2 * 128 : k * 2 * 128 + width] += bias
         relay(b)
 
-        @pl.when(b == 0)
-        def _():
-            for each in sums:
-                each.stage(1)
-
-        @pl.when(b == 1)
-        def _():
-            load_rows.wait()
-            for swap in returns:
-                swap.wait_recv()
-            for q in range(blocks):
-                for s in range(4):
-                    start = q * BLOCK + s * quarter
-                    packed[start : start + quarter, :] = unfold(returned[s, q], width, True)
-            for each in sums:
-                each.rest(2)
-            giving_result.start(packed)
-
-    for c in range(3):
-        late_sum[:, c * width : (c + 1) * width] = dot(packed_in[...], d_rows[c], ((0,), (0,)))
-    for g in range(groups):
-        rows_here = (late_sum[g * held : (g + 1) * held, :] * grad_scale).astype(BF)
-        late_left[g] = rows_here[:, : 2 * width]
-        late_right[g] = rows_here[:, 2 * width :]
-
-    for each in late_sums:
-        each.start()
+    sums[1].stage(1)
     swaps = [
         send(ssent, srecv.at[me], s_sems.at[0, k], s_sems.at[1, k], tensor=peer)
         for k, peer in enumerate((sibling, across, diagonal))
@@ -880,12 +880,17 @@
         swap.start()
     srecv[me] = ssent[...]
 
+    sums[1].rest(2)
+    for each in late_sums:
+        each.stage(1)
     for b in range(blocks):
         near(b).wait()
         far(b).wait_recv()
         total = cols[me, b].astype(F32) + two[b].astype(F32) + three[b].astype(F32)
         packed[b * BLOCK : (b + 1) * BLOCK, :] = unfold(total.astype(BF), width, True)
     giving.start(packed)
+    for each in late_sums:
+        each.rest(2)
 
     for swap in swaps:
         swap.wait_recv()
@@ -901,9 +906,6 @@
     def _(step):
         spread(step).start()
 
-    for stage in range(1, late_sums[0].stages):
-        for each in late_sums:
-            each.stage(stage)
     for k, each in enumerate(sums):
         up_grad[k] = each.collect()
     giving_result.land(landed)

time: 242 us -> 243 us (level)
  no operation moved by 1% of the time
where the time goes in v3:
time: 243 us; the launch traced here: 239 us
  Pallas kernels  227 us (93%)
  local copies, waits for them, and re-layouts  10.6 us (4%)
    pallas_call x3, Pallas kernels, call(): pl.pallas_call(kernel, out_shape=outs, in_specs=specs, out_specs=tuple((p...  227 us
    unnamed x20, local copies, waits for them, and re-layouts  7.91 us

profile of v3, /device:TPU:0, one launch (start us, length us, event | category | flops | bytes accessed | tf_op | source)
XLA Modules:
  0.0 238.7 jit_solution(806368100505329267)
XLA Ops:
  0.6 1.3 reshape.37.seq_row
  1.9 56.2 %shard_map.263 = (bf16[1536,768]{1,0:T(8,128)(2,1)}, bf16[4,3,64,384]{3,2,1,0:T(8,128)(2,1)}, bf16[4,192,768]{2,1,0:T(8,128)(2,1)}, bf16[3,1536,192]{2,1,0:T(8,1...) custom-call(bf16[192,1536]{1,0:T(8,128)(2,1)} %bitcast.27, ...), custom_call_target="tpu_custom_call" | custom-call | tf_op jit(solution)/shard_map/pallas_call | solution.py:73
  58.1 81.8 %shard_map.264 = (bf16[3,4,128,768]{3,2,1,0:T(8,128)(2,1)}, f32[3,128,768]{2,1,0:T(8,128)}, f32[16,768]{1,0:T(8,128)}, bf16[8,96,768]{2,1,0:T(8,128)(2,1)}, bf16...) custom-call(bf16[1536,768]{1,0:T(8,128)(2,1)} %get-tuple-element.37.context, ...), custom_call_target="tpu_custom_call" | custom-call | tf_op jit(solution)/shard_map/pallas_call | solution.py:73
  140.0 88.9 %shard_map.265 = (bf16[192,1536]{1,0:T(8,128)(2,1)}, bf16[192,1536]{1,0:T(8,128)(2,1)}, f32[2,96,768]{2,1,0:T(8,128)}, f32[3,96,192]{2,1,0:T(8,128)}, f32[192,96...) custom-call(bf16[1536,768]{1,0:T(8,128)(2,1)} %bitcast.23, ...), custom_call_target="tpu_custom_call" | custom-call | tf_op jit(solution)/shard_map/pallas_call | solution.py:73
  228.9 0.0 copy-start.2
  228.9 0.0 copy-start.5
  228.9 0.0 copy-start.3
  228.9 0.0 copy-start
  228.9 0.0 copy-start.4
  228.9 0.0 copy-start.1
  228.9 0.9 constant_dynamic-slice_fusion
  229.8 0.5 slice_bitcast_fusion
  230.3 1.9 copy.38
  232.3 1.9 copy.39
  234.2 0.0 copy-done.2
  234.2 0.7 copy.40
  234.9 0.0 copy-done.5
  234.9 0.6 copy.41
  235.5 0.0 copy-done.3
  235.5 0.6 copy.42
  236.1 0.0 copy-done
  236.1 0.8 copy.43
  236.9 0.0 copy-done.4
  236.9 0.6 copy.44
  237.5 0.0 copy-done.1
  237.5 0.7 copy.45
Async XLA Ops:
  228.9 5.3 %copy-start.2 = (f32[3,96,192]{2,1,0:T(8,128)S(1)}, f32[3,96,192]{2,1,0:T(8,128)}, u32[]{:S(2)}) copy-start(f32[3,96,192]{2,1,0:T(8,128)} %get-tuple-element.82) | copy-start | bytes 663556
  228.9 6.0 %copy-start.5 = (f32[2,192]{1,0:T(2,128)S(1)}, f32[2,192]{1,0:T(2,128)}, u32[]{:S(2)}) copy-start(f32[2,192]{1,0:T(2,128)} %get-tuple-element.83) | copy-start | bytes 4612
  228.9 6.6 %copy-start.3 = (f32[192,96]{1,0:T(8,128)S(1)}, f32[192,96]{1,0:T(8,128)}, u32[]{:S(2)}) copy-start(f32[192,96]{1,0:T(8,128)} %get-tuple-element.84) | copy-start | bytes 221188
  228.9 7.2 %copy-start = (f32[2,96,768]{2,1,0:T(8,128)S(1)}, f32[2,96,768]{2,1,0:T(8,128)}, u32[]{:S(2)}) copy-start(f32[2,96,768]{2,1,0:T(8,128)} %get-tuple-element.88) | copy-start | bytes 1769476
  228.9 8.0 %copy-start.4 = (f32[2,768]{1,0:T(2,128)S(1)}, f32[2,768]{1,0:T(2,128)}, u32[]{:S(2)}) copy-start(f32[2,768]{1,0:T(2,128)} %get-tuple-element.89) | copy-start | bytes 18436
  228.9 8.6 %copy-start.1 = (f32[96,768]{1,0:T(8,128)S(1)}, f32[96,768]{1,0:T(8,128)}, u32[]{:S(2)}) copy-start(f32[96,768]{1,0:T(8,128)} %get-tuple-element.59) | copy-start | bytes 884740

commit v4 on v3

--- a/solution.py
+++ b/solution.py
@@ -645,10 +645,7 @@
         add_small(2, d_normed)
 
     def weight_grad(left, right, pieces):
-        span = right.shape[1]
-        for c in range(span // CHUNK):
-            lanes = slice(c * CHUNK, (c + 1) * CHUNK)
-            whole_grad[:, lanes] = dot(left, right[:, lanes], ((0,), (0,)))
+        whole_grad[...] = dot(left, right[...], ((0,), (0,)))
         for g in range(groups):
             rows_here = (whole_grad[g * held : (g + 1) * held, :] * grad_scale).astype(BF)
             for k, target in enumerate(pieces):
@@ -824,15 +821,15 @@
             scored = scores_by_key(keys, queries, slope_of(me * heads + h), distance, same)
             probs = jnp.exp(scored - lse[b, h : h + 1, :])
             d_probs = dot(values, d_rows_out, ((1,), (1,)))
-            d_rows[2, here, lanes] = dot(probs.astype(BF), d_rows_out, ((1,), (0,))).astype(BF)
+            d_rows[here, 2 * width + h * HEAD_DIM : 2 * width + (h + 1) * HEAD_DIM] = dot(probs.astype(BF), d_rows_out, ((1,), (0,))).astype(BF)
             center = jnp.sum(probs * d_probs, axis=0, keepdims=True)
             d_scores = (probs * (d_probs - center)).astype(BF)
-            d_rows[1, here, lanes] = (dot(d_scores, queries, ((1,), (0,))) * (HEAD_DIM**-0.5)).astype(BF)
+            d_rows[here, 1 * width + h * HEAD_DIM : 1 * width + (h + 1) * HEAD_DIM] = (dot(d_scores, queries, ((1,), (0,))) * (HEAD_DIM**-0.5)).astype(BF)
             turned = dot(keys.T, d_scores, ((1,), (0,))) * (HEAD_DIM**-0.5)
-            d_rows[0, here, lanes] = turned.T.astype(BF)
+            d_rows[here, 0 * width + h * HEAD_DIM : 0 * width + (h + 1) * HEAD_DIM] = turned.T.astype(BF)
         last = small.shape[0] - 6
         for k, c in enumerate((0, 2)):
-            bias = jnp.sum(d_rows[c, here, :].astype(F32), axis=0, keepdims=True) * grad_scale
+            bias = jnp.sum(d_rows[here, c * width : (c + 1) * width].astype(F32), axis=0, keepdims=True) * grad_scale
             ssent[last : last + 1, k * 2 * 128 : k * 2 * 128 + width] += bias
         @pl.when(b == 1)
         def _():
@@ -846,8 +843,7 @@
             giving_result.start(packed)
             sums[0].stage(1)
 
-    for c in range(3):
-        late_sum[:, c * width : (c + 1) * width] = dot(packed_in[...], d_rows[c], ((0,), (0,)))
+    late_sum[:, : 3 * width] = dot(packed_in[...], d_rows[...], ((0,), (0,)))
     for g in range(groups):
         rows_here = (late_sum[g * held : (g + 1) * held, :] * grad_scale).astype(BF)
         late_left[g] = rows_here[:, : 2 * width]
@@ -860,10 +856,7 @@
     @pl.loop(0, blocks)
     def _(b):
         here = pl.ds(pl.multiple_of(b * BLOCK, BLOCK), BLOCK)
-        part = dot(d_rows[0, here, :], weight_here[0], ((1,), (0,)))
-        part += dot(d_rows[1, here, :], weight_here[1], ((1,), (0,)))
-        part += dot(d_rows[2, here, :], weight_here[2], ((1,), (0,)))
-        d_part[...] = part
+        d_part[...] = dot(d_rows[here, :], weight_here[...], ((1,), (0,)))
         d_part[pl.ds(pl.multiple_of(me * quarter, quarter), quarter), :] += dh_own[b]
         for u in range(4):
             fold_into(cols, (u, b), d_part[:, u * width : (u + 1) * width].astype(BF), True)
@@ -971,7 +964,7 @@
         number,
         outs,
         [
-            pltpu.VMEM((3, rows, width), BF),
+            pltpu.VMEM((rows, 3 * width), BF),
             pltpu.VMEM((BLOCK, columns), F32),
             pltpu.VMEM((columns, 4 * width), F32),
             pltpu.VMEM((groups, held, 2 * width), BF),
@@ -1062,7 +1055,7 @@
             seq_row,
             context,
             packed_in,
-            weight_turned,
+            weight_turned.reshape(3 * width, columns),
             out_weight,
             gate_grad,
             value_grad,

time: 243 us -> 243 us (level)
  no operation moved by 1% of the time
where the time goes in v4:
time: 243 us; the launch traced here: 239 us
  Pallas kernels  227 us (93%)
  local copies, waits for them, and re-layouts  10.6 us (4%)
    pallas_call x3, Pallas kernels, call(): pl.pallas_call(kernel, out_shape=outs, in_specs=specs, out_specs=tuple((p...  227 us
    unnamed x20, local copies, waits for them, and re-layouts  7.91 us

profile of v4, /device:TPU:0, one launch (start us, length us, event | category | flops | bytes accessed | tf_op | source)
XLA Modules:
  0.0 238.6 jit_solution(10915680889700064174)
XLA Ops:
  0.6 1.3 reshape.40.seq_row
  1.9 55.9 %shard_map.263 = (bf16[1536,768]{1,0:T(8,128)(2,1)}, bf16[4,3,64,384]{3,2,1,0:T(8,128)(2,1)}, bf16[4,192,768]{2,1,0:T(8,128)(2,1)}, bf16[3,1536,192]{2,1,0:T(8,1...) custom-call(bf16[192,1536]{1,0:T(8,128)(2,1)} %bitcast.29, ...), custom_call_target="tpu_custom_call" | custom-call | tf_op jit(solution)/shard_map/pallas_call | solution.py:73
  57.9 82.1 %shard_map.264 = (bf16[3,4,128,768]{3,2,1,0:T(8,128)(2,1)}, f32[3,128,768]{2,1,0:T(8,128)}, f32[16,768]{1,0:T(8,128)}, bf16[8,96,768]{2,1,0:T(8,128)(2,1)}, bf16...) custom-call(bf16[1536,768]{1,0:T(8,128)(2,1)} %get-tuple-element.37.context, ...), custom_call_target="tpu_custom_call" | custom-call | tf_op jit(solution)/shard_map/pallas_call | solution.py:73
  140.0 88.9 %shard_map.265 = (bf16[192,1536]{1,0:T(8,128)(2,1)}, bf16[192,1536]{1,0:T(8,128)(2,1)}, f32[2,96,768]{2,1,0:T(8,128)}, f32[3,96,192]{2,1,0:T(8,128)}, f32[192,96...) custom-call(bf16[1536,768]{1,0:T(8,128)(2,1)} %bitcast.25, ...), custom_call_target="tpu_custom_call" | custom-call | tf_op jit(solution)/shard_map/pallas_call | solution.py:73
  229.0 0.0 copy-start.2
  229.0 0.0 copy-start.5
  229.0 0.0 copy-start.3
  229.0 0.0 copy-start
  229.0 0.0 copy-start.4
  229.0 0.0 copy-start.1
  229.0 0.9 constant_dynamic-slice_fusion
  229.9 0.5 slice_bitcast_fusion
  230.4 1.9 copy.38
  232.3 1.9 copy.39
  234.3 0.0 copy-done.2
  234.3 0.7 copy.40
  235.0 0.0 copy-done.5
  235.0 0.6 copy.41
  235.6 0.0 copy-done.3
  235.6 0.6 copy.42
  236.2 0.0 copy-done
  236.2 0.8 copy.43
  237.0 0.0 copy-done.4
  237.0 0.6 copy.44
  237.6 0.0 copy-done.1
  237.6 0.7 copy.45
Async XLA Ops:
  229.0 5.3 %copy-start.2 = (f32[3,96,192]{2,1,0:T(8,128)S(1)}, f32[3,96,192]{2,1,0:T(8,128)}, u32[]{:S(2)}) copy-start(f32[3,96,192]{2,1,0:T(8,128)} %get-tuple-element.82) | copy-start | bytes 663556
  229.0 6.0 %copy-start.5 = (f32[2,192]{1,0:T(2,128)S(1)}, f32[2,192]{1,0:T(2,128)}, u32[]{:S(2)}) copy-start(f32[2,192]{1,0:T(2,128)} %get-tuple-element.83) | copy-start | bytes 4612
  229.0 6.6 %copy-start.3 = (f32[192,96]{1,0:T(8,128)S(1)}, f32[192,96]{1,0:T(8,128)}, u32[]{:S(2)}) copy-start(f32[192,96]{1,0:T(8,128)} %get-tuple-element.84) | copy-start | bytes 221188
  229.0 7.2 %copy-start = (f32[2,96,768]{2,1,0:T(8,128)S(1)}, f32[2,96,768]{2,1,0:T(8,128)}, u32[]{:S(2)}) copy-start(f32[2,96,768]{2,1,0:T(8,128)} %get-tuple-element.88) | copy-start | bytes 1769476
  229.0 8.0 %copy-start.4 = (f32[2,768]{1,0:T(2,128)S(1)}, f32[2,768]{1,0:T(2,128)}, u32[]{:S(2)}) copy-start(f32[2,768]{1,0:T(2,128)} %get-tuple-element.89) | copy-start | bytes 18436
  229.0 8.6 %copy-start.1 = (f32[96,768]{1,0:T(8,128)S(1)}, f32[96,768]{1,0:T(8,128)}, u32[]{:S(2)}) copy-start(f32[96,768]{1,0:T(8,128)} %get-tuple-element.59) | copy-start | bytes 884740

commit v5 on v4

--- a/solution.py
+++ b/solution.py
@@ -536,9 +536,9 @@
 
 
 def mid_kernel(groups, blocks, grad_scale, context, packed, full_out, up_w, up_bias, down_w, cot_folded, v0, v1, v2, v3, v4, v5,
-               d_low, d_own, small, gate_grad, value_grad, down_grad, folded,
+               d_low, d_own, small, gate_sum, value_grad, down_grad, folded,
                normed_low, slope_term, gelu_term, gated, d_gate, d_value, unit_full, rs_full, unit_own, rs_own, d_mixed,
-               mixed, whole_grad, down_left, down_right, cot_recv,
+               mixed, whole_grad, down_left, down_right, gate_left, gate_right, cot_recv,
                part1, first1, second1, third1, sems1, part2, first2, second2, third2, sems2, sems3, sems4, c_sems,
                vector_rows, *sum_scratch):
     me, sibling, across, diagonal = place_of()
@@ -558,7 +558,9 @@
     back_sum = RowSum(part2, first2, second2, third2, sems2)
     mixed_gather = RowGather(mixed, sems3)
     hidden_gather = RowGather(d_low, sems4)
-    sums = both_ways(groups, (down_left, down_right), sum_scratch)
+    half_scratch = len(sum_scratch) // 2
+    sums = both_ways(groups, (down_left, down_right), sum_scratch[:half_scratch])
+    gate_sums = both_ways(groups, (gate_left, gate_right), sum_scratch[half_scratch:])
     small[...] = jnp.zeros_like(small)
     for k, vector in enumerate((v0, v1, v2, v3, v4, v5)):
         vector_rows[k : k + 1, :] = vector[...].astype(F32).reshape(1, columns)
@@ -680,7 +682,9 @@
     for half in sums:
         half.start()
     finish(0)
-    weight_grad(normed_low[...], d_gate, (gate_grad,))
+    weight_grad(normed_low[...], d_gate, (gate_left, gate_right))
+    for half in gate_sums:
+        half.start()
     if blocks > 1:
         finish(1)
     weight_grad(normed_low[...], d_value, (value_grad,))
@@ -692,17 +696,24 @@
         hidden_gather.relay(b)
     for half in sums:
         half.rest(2)
+    for half in gate_sums:
+        half.stage(1)
     for b in range(blocks):
         hidden_gather.land(b)
     for k, half in enumerate(sums):
         span = half.grads.shape[2]
         down_grad[:, k * span : (k + 1) * span] = half.collect()
+    for half in gate_sums:
+        half.rest(2)
+    for k, half in enumerate(gate_sums):
+        span = half.grads.shape[2]
+        gate_sum[:, k * span : (k + 1) * span] = half.collect()
     for b in range(blocks):
         mixed_gather.end(b)
         hidden_gather.end(b)
     for swap in swaps:
         swap.wait_send()
-    for half in sums:
+    for half in sums + gate_sums:
         half.end()
 
 
@@ -719,7 +730,7 @@
         shape((blocks, 4, quarter, columns), BF),
         shape(own, F32),
         shape((16, columns), F32),
-        shape((groups, held, units), BF),
+        shape((held, units), F32),
         shape((groups, held, units), BF),
         shape((held, units), F32),
         shape(cot_folded.shape, BF),
@@ -744,19 +755,20 @@
             pltpu.VMEM((columns, units), F32),
             pltpu.VMEM((groups, held, units // 2), BF),
             pltpu.VMEM((groups, held, units // 2), BF),
+            pltpu.VMEM((groups, held, units // 2), BF),
+            pltpu.VMEM((groups, held, units // 2), BF),
             pltpu.VMEM(cot_folded.shape, BF),
         ]
         + RowSum.scratch(blocks, quarter, columns)
         + RowSum.scratch(blocks, quarter, columns)
         + [dma((6, blocks)), dma((6, blocks)), dma((2, 3)), pltpu.VMEM((6, columns), F32)]
-        + GroupSum.scratch(groups, held, units // 2)
-        + GroupSum.scratch(groups, held, units // 2),
+        + GroupSum.scratch(groups, held, units // 2) * 4,
         args,
     )
 
 
 def back_kernel(groups, blocks, grad_scale, dh_low, dh_own, qkv, lse, seq_row, context, packed_in, qkv_w,
-                out_w, gate_grad, value_grad, folded, small, taking,
+                out_w, gate_sum, value_grad, folded, small, taking,
                 layer_out, input_grad, up_grad, qkv_grad, out_grad, small_out, qv_out, up_out,
                 d_rows, d_part, late_sum, late_left, late_right, cols, one, two, three, packed, ssent, srecv, swide, x_sems, s_sems, w_sems,
                 start_col, chosen, weight_here, returned, landed, load_sem, r_sems,
@@ -772,13 +784,13 @@
     load_rows = pltpu.make_async_copy(taking, chosen, load_sem.at[1])
     load_rows.start()
     enter([sibling, across, diagonal], groups)
-    half_scratch = len(sum_scratch) // 2
-    sums = both_ways(groups, (gate_grad, value_grad), sum_scratch[:half_scratch], False)
-    late_sums = both_ways(groups, (late_left, late_right), sum_scratch[half_scratch:])
+    part_scratch = len(sum_scratch) // 3
+    value_sum = GroupSum(groups, value_grad, sum_scratch[:part_scratch], False)
+    late_sums = both_ways(groups, (late_left, late_right), sum_scratch[part_scratch:])
     giving = GiveBack(groups, rows, width, chosen, sent, recv, a_sems)
     giving_result = GiveBack(groups, rows, width, chosen, sent2, recv5, a_sems2)
-    for each in sums:
-        each.start()
+    value_sum.start()
+    up_grad[0] = gate_sum[...]
     returns = [
         send(folded.at[peer], returned.at[me], r_sems.at[0, k], r_sems.at[1, k], tensor=peer)
         for k, peer in enumerate((across, diagonal, sibling))
@@ -841,7 +853,7 @@
                     start = q * BLOCK + s * quarter
                     packed[start : start + quarter, :] = unfold(returned[s, q], width, True)
             giving_result.start(packed)
-            sums[0].stage(1)
+            value_sum.stage(1)
 
     late_sum[:, : 3 * width] = dot(packed_in[...], d_rows[...], ((0,), (0,)))
     for g in range(groups):
@@ -851,7 +863,7 @@
 
     for each in late_sums:
         each.start()
-    sums[0].rest(2)
+    value_sum.rest(2)
 
     @pl.loop(0, blocks)
     def _(b):
@@ -864,7 +876,6 @@
         near(b).start()
         relay(b)
 
-    sums[1].stage(1)
     swaps = [
         send(ssent, srecv.at[me], s_sems.at[0, k], s_sems.at[1, k], tensor=peer)
         for k, peer in enumerate((sibling, across, diagonal))
@@ -873,7 +884,6 @@
         swap.start()
     srecv[me] = ssent[...]
 
-    sums[1].rest(2)
     for each in late_sums:
         each.stage(1)
     for b in range(blocks):
@@ -899,8 +909,7 @@
     def _(step):
         spread(step).start()
 
-    for k, each in enumerate(sums):
-        up_grad[k] = each.collect()
+    up_grad[1] = value_sum.collect()
     giving_result.land(landed)
     layer_out[...] = landed[...].T
 
@@ -933,7 +942,7 @@
         far(b).wait_send()
     for copy in returns:
         copy.wait_send()
-    for each in sums + late_sums:
+    for each in [value_sum] + late_sums:
         each.end()
 
     @pl.loop(1, groups)
@@ -942,7 +951,7 @@
 
 
 def back(groups, grad_scale, args, small, number):
-    dh_low, qkv, qkv_w, grad, folded = args[0], args[2], args[7], args[9], args[11]
+    dh_low, qkv, qkv_w, grad, folded = args[0], args[2], args[7], args[10], args[11]
     rows, columns = dh_low.shape
     width = qkv.shape[2]
     held, units = grad.shape[1:]
@@ -990,7 +999,7 @@
         ]
         + GiveBack.scratch(groups, rows, width)
         + GiveBack.scratch(groups, rows, width)
-        + GroupSum.scratch(groups, held, units) * 2
+        + GroupSum.scratch(groups, held, units)
         + GroupSum.scratch(groups, held, 2 * width) * 2,
         args,
         apart=(7, 13),
@@ -1024,7 +1033,7 @@
     packed_in, cot_folded, full_out, qkv_rows, log_total, context, wide_context, taking = front(
         groups, (tokens.T, cotangent.T, row_place, seq_row, weight_turned, qv_bias, out_weight), 0
     )
-    d_low, d_own, small, gate_grad, value_grad, down_grad, folded = mid(
+    d_low, d_own, small, gate_sum, value_grad, down_grad, folded = mid(
         groups,
         grad_scale,
         (
@@ -1057,7 +1066,7 @@
             packed_in,
             weight_turned.reshape(3 * width, columns),
             out_weight,
-            gate_grad,
+            gate_sum,
             value_grad,
             folded,
             small,

time: 243 us -> 242 us (level)
  the two profiles are of different devices: /device:TPU:0 before, /device:TPU:28 now
where the time goes in v5:
time: 242 us; the launch traced here: 238 us
  Pallas kernels  226 us (93%)
  local copies, waits for them, and re-layouts  10.6 us (4%)
    pallas_call x3, Pallas kernels, call(): pl.pallas_call(kernel, out_shape=outs, in_specs=specs, out_specs=tuple((p...  226 us
    unnamed x20, local copies, waits for them, and re-layouts  7.91 us

profile of v5, /device:TPU:28, one launch (start us, length us, event | category | flops | bytes accessed | tf_op | source)
XLA Modules:
  0.0 238.1 jit_solution(5252043712200993053)
XLA Ops:
  0.6 1.3 reshape.40.seq_row
  1.9 56.9 %shard_map.263 = (bf16[1536,768]{1,0:T(8,128)(2,1)}, bf16[4,3,64,384]{3,2,1,0:T(8,128)(2,1)}, bf16[4,192,768]{2,1,0:T(8,128)(2,1)}, bf16[3,1536,192]{2,1,0:T(8,1...) custom-call(bf16[192,1536]{1,0:T(8,128)(2,1)} %bitcast.29, ...), custom_call_target="tpu_custom_call" | custom-call | tf_op jit(solution)/shard_map/pallas_call | solution.py:73
  58.8 89.0 %shard_map.264 = (bf16[3,4,128,768]{3,2,1,0:T(8,128)(2,1)}, f32[3,128,768]{2,1,0:T(8,128)}, f32[16,768]{1,0:T(8,128)}, f32[96,768]{1,0:T(8,128)}, bf16[8,96,768]...) custom-call(bf16[1536,768]{1,0:T(8,128)(2,1)} %get-tuple-element.37.context, ...), custom_call_target="tpu_custom_call" | custom-call | tf_op jit(solution)/shard_map/pallas_call | solution.py:73
  147.8 80.5 %shard_map.265 = (bf16[192,1536]{1,0:T(8,128)(2,1)}, bf16[192,1536]{1,0:T(8,128)(2,1)}, f32[2,96,768]{2,1,0:T(8,128)}, f32[3,96,192]{2,1,0:T(8,128)}, f32[192,96...) custom-call(bf16[1536,768]{1,0:T(8,128)(2,1)} %bitcast.25, ...), custom_call_target="tpu_custom_call" | custom-call | tf_op jit(solution)/shard_map/pallas_call | solution.py:73
  228.4 0.0 copy-start.2
  228.4 0.0 copy-start.5
  228.4 0.0 copy-start.3
  228.4 0.0 copy-start
  228.4 0.0 copy-start.4
  228.4 0.0 copy-start.1
  228.4 0.8 constant_dynamic-slice_fusion
  229.3 0.5 slice_bitcast_fusion
  229.8 1.9 copy.38
  231.7 1.9 copy.39
  233.6 0.0 copy-done.2
  233.6 0.7 copy.40
  234.3 0.0 copy-done.5
  234.4 0.6 copy.41
  234.9 0.0 copy-done.3
  234.9 0.6 copy.42
  235.6 0.0 copy-done
  235.6 0.8 copy.43
  236.4 0.0 copy-done.4
  236.4 0.6 copy.44
  237.0 0.0 copy-done.1
  237.0 0.7 copy.45
Async XLA Ops:
  228.4 5.3 %copy-start.2 = (f32[3,96,192]{2,1,0:T(8,128)S(1)}, f32[3,96,192]{2,1,0:T(8,128)}, u32[]{:S(2)}) copy-start(f32[3,96,192]{2,1,0:T(8,128)} %get-tuple-element.82) | copy-start | bytes 663556
  228.4 6.0 %copy-start.5 = (f32[2,192]{1,0:T(2,128)S(1)}, f32[2,192]{1,0:T(2,128)}, u32[]{:S(2)}) copy-start(f32[2,192]{1,0:T(2,128)} %get-tuple-element.83) | copy-start | bytes 4612
  228.4 6.6 %copy-start.3 = (f32[192,96]{1,0:T(8,128)S(1)}, f32[192,96]{1,0:T(8,128)}, u32[]{:S(2)}) copy-start(f32[192,96]{1,0:T(8,128)} %get-tuple-element.84) | copy-start | bytes 221188
  228.4 7.2 %copy-start = (f32[2,96,768]{2,1,0:T(8,128)S(1)}, f32[2,96,768]{2,1,0:T(8,128)}, u32[]{:S(2)}) copy-start(f32[2,96,768]{2,1,0:T(8,128)} %get-tuple-element.88) | copy-start | bytes 1769476
  228.4 8.0 %copy-start.4 = (f32[2,768]{1,0:T(2,128)S(1)}, f32[2,768]{1,0:T(2,128)}, u32[]{:S(2)}) copy-start(f32[2,768]{1,0:T(2,128)} %get-tuple-element.89) | copy-start | bytes 18436
  228.4 8.6 %copy-start.1 = (f32[96,768]{1,0:T(8,128)S(1)}, f32[96,768]{1,0:T(8,128)}, u32[]{:S(2)}) copy-start(f32[96,768]{1,0:T(8,128)} %get-tuple-element.59) | copy-start | bytes 884740
